TPU v7x, 256 devices: a whole 4x4x8 slice. The times are simulated.
256 devices in a mesh: row: 8 (over z_lo, core), col: 32 (over z_hi, x, y).
Axes of the slice: x: 4, y: 4, z: 8 (z_hi: 2, z_lo: 4; z = z_hi * 4 + z_lo), core: 2. Of those that a mesh axis runs over, the one named last changes fastest.
Arguments:
- movie: bfloat16 [512, 2048, 256], P('row', 'col'), may hold values from 0 to 1.5
- footprints: float32 [8, 32, 12, 4096], P('row', 'col'), may hold values from 0.05 to 1
- anchors: int32 [8, 32, 12, 2], P('row', 'col'), may hold values from 0 to 63, as said below
- groups: int32 [8, 32, 12], P('row', 'col'), may hold values from 0 to 3, as said below
- counts: int32 [8, 32], P('row', 'col'), may hold values from 1 to 12, as said below
- temporal: float32 [8, 32, 12, 256], P('row', 'col'), may hold values from 0.2 to 2
- back_spatial: bfloat16 [2, 512, 2048], P(None, 'row', 'col'), may hold values from 0 to 0.5
- back_temporal: float32 [2, 256], replicated, may hold values from 0.5 to 1
- window: int32 [2], replicated, may hold values from 0 to 256, as said below
Outputs:
- new_footprints: float32 [8, 32, 12, 4096], P('row', 'col')
- new_traces: float32 [8, 32, 12, 256], P('row', 'col')
Inputs may be any that keep to these rules, and one draw needn't show every extreme that they name: `anchors`: a block's anchor lies in its tile; on the last tile row the row offset is at most 0, on the last tile column the column offset at most 0. `counts`: slots below the count are live, the others are ignored; some tile has 12 live slots. `groups`: every tile has exactly 3 slots, live or not, in each group. window[0] is at most 64 and window[1] at least 192.
All inputs are finite; a program needn't handle non-finite values.
Results may differ from a plain program's by a relative error of at most 0.00084.
Values may be sent and summed in bfloat16 or wider, within the bound.
A program may use at most 64 MiB of HBM per device.

v0:
```python
import jax
import jax.numpy as jnp
from jax import lax
from jax.sharding import PartitionSpec as P

FP = 64
GROUPS = 4


exact_mode = lax.Precision.HIGHEST


def padded(cells, sides, width):
    for axis, dim in sides:
        count = lax.axis_size(axis)
        ends = count - 1
        head = lax.slice_in_dim(cells, 0, width, axis=dim)
        tail = lax.slice_in_dim(cells, cells.shape[dim] - width, cells.shape[dim], axis=dim)
        cells = jnp.concatenate(
            [
                lax.ppermute(tail, axis, [(i, (i + 1) % count) for i in range(ends)]),
                cells,
                lax.ppermute(head, axis, [((i + 1) % count, i) for i in range(ends)]),
            ],
            axis=dim,
        )
    return cells


def shifted(value, axis, steps):
    count = lax.axis_size(axis)
    initial, last = (max(0, -steps), min(count, count - steps))
    return lax.ppermute(value, axis, [(source, source + steps) for source in range(initial, last)])


def near_traces(traces):
    return padded(traces[None, None], (("row", 0), ("col", 1)), 1)


def selector(starts, extent):
    places = jnp.arange(extent, dtype=jnp.int32)[None, :, None]
    offsets = jnp.arange(FP, dtype=jnp.int32)[None, None, :]
    return (places == starts[:, None, None] + offsets).astype(jnp.float32)


def on_device(
    movie, footprints, anchors, groups, counts, temporal, back_spatial, back_temporal, window
):
    tile_rows, tile_cols, frame_count = movie.shape
    slot_count = footprints.shape[2]
    pixels = tile_rows * tile_cols
    ext_rows = tile_rows + FP
    ext_cols = tile_cols + FP
    ext_pixels = ext_rows * ext_cols
    count_near = 9 * slot_count
    count_tile = 4 * slot_count
    slot_ids = jnp.arange(slot_count, dtype=jnp.int32)
    living = (slot_ids < counts[0, 0]).astype(jnp.float32)
    shapes = footprints[0, 0] * living[:, None]
    labels = jnp.concatenate(
        [
            anchors[0, 0].astype(jnp.float32),
            groups[0, 0][:, None].astype(jnp.float32),
            living[:, None],
        ],
        axis=1,
    )
    near_shapes, near_labels = (
        padded(shapes[None, None], (("row", 0), ("col", 1)), 1),
        padded(labels[None, None], (("row", 0), ("col", 1)), 1),
    )
    tile_step = jnp.arange(3, dtype=jnp.int32) - 1
    top_rows = (
        near_labels[..., 0].astype(jnp.int32) + (tile_step * tile_rows)[:, None, None]
    ).reshape(count_near)
    left_cols = (
        near_labels[..., 1].astype(jnp.int32) + (tile_step * tile_cols)[None, :, None]
    ).reshape(count_near)
    near_groups = near_labels[..., 2].astype(jnp.int32)
    tile_groups = near_groups[:2, :2].reshape(count_tile)
    tile_living = near_labels[:2, :2, :, 3].reshape(count_tile)
    row_pick = selector(top_rows, ext_rows)
    col_pick = selector(left_cols, ext_cols)
    sectioned = jnp.einsum(
        "nyi,nij->nyj", row_pick, near_shapes.reshape(count_near, FP, FP), precision=exact_mode
    )
    canvas = jnp.einsum("nyj,nxj->nyx", sectioned, col_pick, precision=exact_mode)
    flattened = canvas.reshape(count_near, ext_pixels)
    owned = flattened[4 * slot_count : 5 * slot_count]
    coupling = jnp.dot(owned, flattened.T, precision=exact_mode)
    self_weight = jnp.diagonal(coupling[:, 4 * slot_count : 5 * slot_count])
    safe_self = jnp.where(living > 0, self_weight, 1.0)
    tile_canvas = canvas.reshape(3, 3, slot_count, ext_rows, ext_cols)[
        :2, :2, :, :tile_rows, :tile_cols
    ].reshape(count_tile, pixels)
    row_select = row_pick.reshape(3, 3, slot_count, ext_rows, FP)[:2, :2, :, :tile_rows].reshape(
        count_tile, tile_rows, FP
    )
    col_select = col_pick.reshape(3, 3, slot_count, ext_cols, FP)[:2, :2, :, :tile_cols].reshape(
        count_tile, tile_cols, FP
    )
    back_tile = back_spatial.astype(jnp.float32).reshape(2, pixels)
    movie_flat = movie.reshape(pixels, frame_count)
    loadings = jnp.dot(tile_canvas, back_tile.T, precision=exact_mode)
    shares = jnp.dot(
        tile_canvas.astype(jnp.bfloat16), movie_flat, preferred_element_type=jnp.float32
    )
    shares = (shares - jnp.dot(loadings, back_temporal, precision=exact_mode)).reshape(
        2, 2, slot_count, frame_count
    )
    from_east = shifted(shares[:, 0], "col", -1)
    column_sum = shares[:, 1] + from_east
    from_south = shifted(column_sum[0], "row", -1)
    drives = column_sum[1] + from_south
    moments = jnp.arange(frame_count, dtype=jnp.int32)
    inside = ((moments >= window[0]) & (moments < window[1])).astype(jnp.float32)
    row_cover = jnp.sum(row_select, axis=2)
    col_cover = jnp.sum(col_select, axis=2)
    cover = (row_cover[:, :, None] * col_cover[:, None, :]).reshape(
        count_tile, pixels
    ) * tile_living[:, None]
    traces = temporal[0, 0]
    nearby = near_traces(traces)
    first_near = nearby
    for step in range(GROUPS):
        if step > 0:
            nearby = near_traces(traces)
        temporal_coupled = jnp.dot(
            coupling, nearby.reshape(count_near, frame_count), precision=exact_mode
        )
        temporal_chosen = living * (groups[0, 0] == step).astype(jnp.float32)
        temporal_updated = jnp.maximum(
            traces + (drives - temporal_coupled) / safe_self[:, None], 0.0
        )
        traces = jnp.where(temporal_chosen[:, None] > 0, temporal_updated, traces)
    tile_traces = first_near[:2, :2].reshape(count_tile, frame_count)
    weighted = tile_traces * inside[None, :]
    intersection_time = jnp.dot(weighted, weighted.T, precision=exact_mode)
    safe_mass = jnp.where(tile_living > 0, jnp.diagonal(intersection_time), 1.0)
    back_loads = jnp.dot(weighted, back_temporal.T, precision=exact_mode)
    target = lax.dot_general(
        weighted.astype(jnp.bfloat16),
        movie_flat,
        (((1,), (1,)), ((), ())),
        preferred_element_type=jnp.float32,
    )
    target = target - jnp.dot(back_loads, back_tile, precision=exact_mode)
    values = tile_canvas
    for step in range(GROUPS):
        coupled = jnp.dot(intersection_time, values, precision=exact_mode)
        chosen = cover * (tile_groups == step).astype(jnp.float32)[:, None]
        updated = jnp.maximum(values + (target - coupled) / safe_mass[:, None], 0.0)
        values = jnp.where(chosen > 0, updated, values)
    lifted = jnp.einsum(
        "nyi,nyx->nix",
        row_select,
        values.reshape(count_tile, tile_rows, tile_cols),
        precision=exact_mode,
    )
    blocks = jnp.einsum("nix,nxj->nij", lifted, col_select, precision=exact_mode).reshape(
        2, 2, slot_count, FP * FP
    )
    from_east = shifted(blocks[:, 0], "col", -1)
    column_sum = blocks[:, 1] + from_east
    from_south = shifted(column_sum[0], "row", -1)
    new_shapes = column_sum[1] + from_south
    return (new_shapes[None, None], traces[None, None])


def solution(mesh):
    return jax.shard_map(
        on_device,
        mesh=mesh,
        in_specs=(
            P("row", "col", None),
            P("row", "col", None, None),
            P("row", "col", None, None),
            P("row", "col", None),
            P("row", "col"),
            P("row", "col", None, None),
            P(None, "row", "col"),
            P(),
            P(),
        ),
        out_specs=(P("row", "col", None, None), P("row", "col", None, None)),
        check_vma=False,
    )
```

profile of v0, /device:TPU:129, one launch (start us, length us, event | category | flops | bytes accessed | tf_op | source)
XLA Modules:
  0.0 276.7 jit_solution(16003865614205424393)
XLA Ops:
  2.8 3.2 %collective-permute-start = (f32[1,1,12,4]{2,3,1,0:T(4,128)S(1)}, f32[1,1,12,4]{2,3,1,0:T(4,128)S(1)}, u32[]{:S(2)}, u32[]{:S(2)}) collective-permute-start(f32[1,1,12,4]{2,3,1,0:T(4,128)S(1)} %maximum_bitcast_fusion), channel_id=1, source_target_pairs={{0,32},{32,64},{64,96},{96,128},{128,160},{160,192},{192,224},{1,3... | collective-permute-start | bytes 584 | tf_op jit(solution)/shard_map/ppermute | solution.py:21
  6.0 1.9 collective-permute-start.1
  8.0 1.1 broadcast_multiply_fusion.1
  9.1 3.6 %collective-permute-start.4 = (f32[1,1,12,4096]{3,1,2,0:T(1,128)S(1)}, f32[1,1,12,4096]{3,1,2,0:T(1,128)S(1)}, u32[]{:S(2)}, u32[]{:S(2)}) collective-permute-start(f32[1,1,12,4096]{3,1,2,0:T(1,128)S(1)} %broadcast_multiply_fusion.1), channel_id=1, source_target_pairs={{0,32},{32,64},{64,96},{96,128},{128,160},{160,192},{192,224},{1,3... | collective-permute-start | bytes 589832 | tf_op jit(solution)/shard_map/ppermute | solution.py:21
  12.8 1.9 collective-permute-start.5
  14.7 3.6 %collective-permute-start.8 = (f32[1,1,12,256]{3,1,2,0:T(1,128)}, f32[1,1,12,256]{3,1,2,0:T(1,128)S(1)}, u32[]{:S(2)}, u32[]{:S(2)}) collective-permute-start(f32[1,1,12,256]{3,1,2,0:T(1,128)} %param.14), channel_id=1, source_target_pairs={{0,32},{32,64},{64,96},{96,128},{128,160},{160,192},{192,224},{1,3... | collective-permute-start | bytes 36872 | tf_op jit(solution)/shard_map/ppermute | solution.py:21
  18.4 1.2 fusion.53
  19.6 1.3 fusion.60
  20.9 1.2 and_convert_fusion
  22.2 3.2 %collective-permute-start.2 = (f32[3,1,12,4]{2,3,1,0:T(4,128)S(1)}, f32[3,1,12,4]{2,3,1,0:T(4,128)S(1)}, u32[]{:S(2)}, u32[]{:S(2)}) collective-permute-start(f32[3,1,12,4]{2,3,1,0:T(4,128)S(1)} %pad_maximum_fusion.10), channel_id=1, source_target_pairs={{0,1},{1,2},{2,3},{3,4},{4,5},{5,6},{6,7},{7,8},{8,9},{9,10},{10,1... | collective-permute-start | bytes 1736 | tf_op jit(solution)/shard_map/ppermute | solution.py:21
  25.4 10.2 %collective-permute-start.3 = (f32[3,1,12,4]{2,3,1,0:T(4,128)S(1)}, f32[3,1,12,4]{2,3,1,0:T(4,128)S(1)}, u32[]{:S(2)}, u32[]{:S(2)}) collective-permute-start(f32[3,1,12,4]{2,3,1,0:T(4,128)S(1)} %pad_maximum_fusion.10), channel_id=1, source_target_pairs={{1,0},{2,1},{3,2},{4,3},{5,4},{6,5},{7,6},{8,7},{9,8},{10,9},{11,1... | collective-permute-start | bytes 1736 | tf_op jit(solution)/shard_map/ppermute | solution.py:23
  36.8 1.9 collective-permute-start.9
  39.6 1.3 add_compare_fusion.1
  42.6 1.7 broadcast_multiply_fusion
  44.3 1.9 collective-permute-start.10
  46.3 2.8 %mul.125 = f32[48,4096]{1,0:T(8,128)} reshape(f32[48,64,64]{2,1,0:T(8,128)} %broadcast_multiply_fusion) | data formatting | bytes 1572864 | tf_op jit(solution)/shard_map/mul | solution.py:119
  51.7 11.5 %collective-permute-start.15 = (f32[3,1,12,256]{3,1,2,0:T(1,128)S(1)}, f32[3,1,12,256]{3,1,2,0:T(1,128)S(1)}, u32[]{:S(2)}, u32[]{:S(2)}) collective-permute-start(f32[3,1,12,256]{3,1,2,0:T(1,128)S(1)} %constant_dynamic-update-slice_fusion), channel_id=1, source_target_pairs={{1,0},{2,1},{3,2},{4,3},{5,4},{6,5},{7,6},{8,7},{9,8},{10,9},{11,1... | collective-permute-start | bytes 110600 | tf_op jit(solution)/shard_map/ppermute | solution.py:23
  63.5 1.0 gather_fusion
  65.2 1.4 pad_maximum_fusion.1
  66.6 1.9 collective-permute-start.6
  68.5 11.5 %collective-permute-start.7 = (f32[3,1,12,4096]{3,1,2,0:T(1,128)}, f32[3,1,12,4096]{3,1,2,0:T(1,128)}, u32[]{:S(2)}, u32[]{:S(2)}) collective-permute-start(f32[3,1,12,4096]{3,1,2,0:T(1,128)} %pad_maximum_fusion.1), channel_id=1, source_target_pairs={{1,0},{2,1},{3,2},{4,3},{5,4},{6,5},{7,6},{8,7},{9,8},{10,9},{11,1... | collective-permute-start | bytes 1769480 | tf_op jit(solution)/shard_map/ppermute | solution.py:23
  81.6 1.4 convolution_subtract_fusion.4
  83.0 8.8 %collective-permute-done.6 = f32[3,1,12,4096]{3,1,2,0:T(1,128)} collective-permute-done((f32[3,1,12,4096]{3,1,2,0:T(1,128)}, f32[3,1,12,4096]{3,1,2,0:T(1,128)}, u32[]{:S(2)}, u32[]{:S(2)}) %collective-permute-start.6) | collective-permute-done | bytes 589856 | tf_op jit(solution)/shard_map/ppermute | solution.py:21
  91.8 1.6 collective-permute-done.7
  93.5 2.8 %pad_maximum_fusion = f32[3,3,12,4096]{3,1,2,0:T(4,128)S(1)} fusion(f32[3,1,12,4096]{3,1,2,0:T(1,128)} %collective-permute-done.7, f32[1,1,12,4096]{3,1,2,0:T(1,128)S(1)} %collective-permute-done.5, f32[1,1,12,4096]{3,1,2,0:T(1,128)S(1)} %broadcast_multiply_fusion.1, f32[1,1,12,4096]{3,1,2,0:T(1,128)S(1)} %collective-permute-done.4, ...), kind=kLoop, calls=%fused_computation.29 | loop fusion | flops 1769472 | bytes 3538944 | tf_op jit(solution)/shard_map/concatenate | solution.py:19
  96.3 2.5 copy.31
  98.8 4.0 %reshape.328 = f32[108,64,64]{2,1,0:T(8,128)} reshape(f32[3,3,12,4096]{3,2,1,0:T(8,128)} %copy.31) | data formatting | bytes 3538944 | tf_op jit(solution)/shard_map/reshape | solution.py:85
  102.8 6.6 %fusion.18 = f32[108,128,64]{1,2,0:T(8,128)S(1)} fusion(f32[108,64,64]{2,1,0:T(8,128)} %reshape.328, s32[108,64]{1,0:T(8,128)S(1)} %copy-done.7), kind=kOutput, calls=%fused_computation.27 | convolution fusion | flops 680361984 | bytes 5336064 | tf_op jit(solution)/shard_map/nyi,nij->nyj/dot_general | solution.py:84
  109.3 7.5 %fusion.19 = f32[108,128,128]{2,1,0:T(8,128)S(1)} fusion(f32[108,128,64]{1,2,0:T(8,128)S(1)} %fusion.18, s32[108,64]{1,0:T(8,128)S(1)} %iota_add_fusion.2), kind=kOutput, calls=%fused_computation.28 | convolution fusion | flops 1359839232 | bytes 10644480 | tf_op jit(solution)/shard_map/nyj,nxj->nyx/dot_general | solution.py:87
  116.9 1.3 slice.102
  118.3 9.0 %fusion.39 = f32[12,108]{1,0:T(8,128)S(1)} fusion(f32[108,128,128]{2,1,0:T(8,128)S(1)} %fusion.19, f32[12,128,128]{2,1,0:T(8,128)S(1)} %slice.111), kind=kOutput, calls=%fused_computation.58 | convolution fusion | flops 254803968 | bytes 7869504 | tf_op jit(solution)/shard_map/dot_general | solution.py:90
  127.3 2.8 %reshape.330 = f32[48,4096]{1,0:T(8,128)} reshape(f32[2,2,12,64,64]{4,3,2,1,0:T(8,128)} %slice.102) | data formatting | bytes 1572864 | tf_op jit(solution)/shard_map/reshape | solution.py:95
  130.1 1.6 fusion.66
  131.7 1.4 convert_element_type.176
  133.1 1.5 fusion.65
  135.0 12.6 %collective-permute-start.13 = (f32[2,12,256]{2,1,0:T(8,128)S(1)}, f32[2,12,256]{2,1,0:T(8,128)S(1)}, u32[]{:S(2)}, u32[]{:S(2)}) collective-permute-start(f32[2,12,256]{2,1,0:T(8,128)S(1)} %slice_bitcast_fusion.4), channel_id=1, source_target_pairs={{1,0},{2,1},{3,2},{4,3},{5,4},{6,5},{7,6},{8,7},{9,8},{10,9},{11,1... | collective-permute-start | bytes 73736 | tf_op jit(solution)/shard_map/ppermute | solution.py:33
  147.6 2.3 fusion.5
  151.0 1.8 fusion.13
  153.6 2.7 collective-permute-start.14
  156.3 14.6 %collective-permute-done.14 = f32[12,256]{1,0:T(8,128)S(1)} collective-permute-done((f32[12,256]{1,0:T(8,128)S(1)}, f32[12,256]{1,0:T(8,128)S(1)}, u32[]{:S(2)}, u32[]{:S(2)}) %collective-permute-start.14) | collective-permute-done | bytes 12320 | tf_op jit(solution)/shard_map/ppermute | solution.py:33
  171.1 1.9 collective-permute-start.16
  173.0 2.4 collective-permute-start.17
  175.4 3.7 %fusion.17 = f32[48,4096]{1,0:T(8,128)} fusion(f32[48,4096]{1,0:T(8,128)} %fusion.13, f32[48,4096]{1,0:T(8,128)} %convolution_subtract_fusion.4, f32[48,48]{1,0:T(8,128)S(1)} %fusion.62, f32[48,4096]{1,0:T(8,128)} %mul.125, f32[48]{0:T(128)S(1)} %copy-done.21, f32[48]{0:T(128)S(1)} %copy-done.17, f32[48]{0:T(128)S(1)} %copy-done.16), kind=kOutput, calls=%fused_computation.23 | convolution fusion | flops 114819072 | bytes 3155520 | tf_op jit(solution)/shard_map/dot_general | solution.py:150
  179.1 3.0 %reshape.334 = f32[48,64,64]{2,1,0:T(8,128)} reshape(f32[48,4096]{1,0:T(8,128)} %fusion.17) | data formatting | bytes 1572864 | tf_op jit(solution)/shard_map/reshape | solution.py:157
  182.1 1.9 collective-permute-start.18
  184.1 11.5 %collective-permute-start.19 = (f32[3,1,12,256]{3,2,1,0:T(8,128)S(1)}, f32[3,1,12,256]{3,2,1,0:T(8,128)S(1)}, u32[]{:S(2)}, u32[]{:S(2)}) collective-permute-start(f32[3,1,12,256]{3,2,1,0:T(8,128)S(1)} %pad_maximum_fusion.7), channel_id=1, source_target_pairs={{1,0},{2,1},{3,2},{4,3},{5,4},{6,5},{7,6},{8,7},{9,8},{10,9},{11,1... | collective-permute-start | bytes 110600 | tf_op jit(solution)/shard_map/ppermute | solution.py:23
  195.6 3.6 %fusion.63 = f32[48,64,64]{2,1,0:T(8,128)} fusion(pred[48,64,64]{1,2,0:T(32,128)(4,1)S(1)} %bitcast.131, f32[48,64,64]{2,1,0:T(8,128)} %reshape.334), kind=kOutput, calls=%fused_computation.144 | convolution fusion | flops 150994944 | bytes 1769472 | tf_op jit(solution)/shard_map/nyi,nyx->nix/dot_general | solution.py:154
  199.4 3.7 %collective-permute-start.20 = (f32[1,1,12,256]{3,2,1,0:T(8,128)S(1)}, f32[1,1,12,256]{3,2,1,0:T(8,128)S(1)}, u32[]{:S(2)}, u32[]{:S(2)}) collective-permute-start(f32[1,1,12,256]{3,2,1,0:T(8,128)S(1)} %bitcast.140), channel_id=1, source_target_pairs={{0,32},{32,64},{64,96},{96,128},{128,160},{160,192},{192,224},{1,3... | collective-permute-start | bytes 36872 | tf_op jit(solution)/shard_map/ppermute | solution.py:21
  203.1 1.9 collective-permute-start.21
  205.1 3.6 %fusion.64 = f32[48,64,64]{2,1,0:T(8,128)} fusion(f32[48,64,64]{2,1,0:T(8,128)} %fusion.63, pred[48,64,64]{2,1,0:T(32,128)(4,1)S(1)} %bitcast.130), kind=kOutput, calls=%fused_computation.145 | convolution fusion | flops 150994944 | bytes 1769472 | tf_op jit(solution)/shard_map/nix,nxj->nij/dot_general | solution.py:160
  208.7 1.9 reshape.336
  210.6 1.9 collective-permute-start.22
  212.6 11.5 %collective-permute-start.23 = (f32[3,1,12,256]{3,2,1,0:T(8,128)S(1)}, f32[3,1,12,256]{3,2,1,0:T(8,128)S(1)}, u32[]{:S(2)}, u32[]{:S(2)}) collective-permute-start(f32[3,1,12,256]{3,2,1,0:T(8,128)S(1)} %pad_maximum_fusion.8), channel_id=1, source_target_pairs={{1,0},{2,1},{3,2},{4,3},{5,4},{6,5},{7,6},{8,7},{9,8},{10,9},{11,1... | collective-permute-start | bytes 110600 | tf_op jit(solution)/shard_map/ppermute | solution.py:23
  224.9 2.6 collective-permute-start.11
  227.7 4.5 %collective-permute-start.24 = (f32[1,1,12,256]{3,2,1,0:T(8,128)S(1)}, f32[1,1,12,256]{3,2,1,0:T(8,128)S(1)}, u32[]{:S(2)}, u32[]{:S(2)}) collective-permute-start(f32[1,1,12,256]{3,2,1,0:T(8,128)S(1)} %bitcast.132), channel_id=1, source_target_pairs={{0,32},{32,64},{64,96},{96,128},{128,160},{160,192},{192,224},{1,3... | collective-permute-start | bytes 36872 | tf_op jit(solution)/shard_map/ppermute | solution.py:21
  232.2 1.9 collective-permute-start.25
  234.2 3.9 %collective-permute-done.24 = f32[1,1,12,256]{3,2,1,0:T(8,128)S(1)} collective-permute-done((f32[1,1,12,256]{3,2,1,0:T(8,128)S(1)}, f32[1,1,12,256]{3,2,1,0:T(8,128)S(1)}, u32[]{:S(2)}, u32[]{:S(2)}) %collective-permute-start.24) | collective-permute-done | bytes 12320 | tf_op jit(solution)/shard_map/ppermute | solution.py:21
  238.0 13.8 %collective-permute-done.25 = f32[1,1,12,256]{3,2,1,0:T(8,128)S(1)} collective-permute-done((f32[1,1,12,256]{3,2,1,0:T(8,128)S(1)}, f32[1,1,12,256]{3,2,1,0:T(8,128)S(1)}, u32[]{:S(2)}, u32[]{:S(2)}) %collective-permute-start.25) | collective-permute-done | bytes 12320 | tf_op jit(solution)/shard_map/ppermute | solution.py:23
  251.8 1.9 collective-permute-start.26
  253.8 11.5 %collective-permute-start.27 = (f32[3,1,12,256]{3,2,1,0:T(8,128)S(1)}, f32[3,1,12,256]{3,2,1,0:T(8,128)S(1)}, u32[]{:S(2)}, u32[]{:S(2)}) collective-permute-start(f32[3,1,12,256]{3,2,1,0:T(8,128)S(1)} %pad_maximum_fusion.9), channel_id=1, source_target_pairs={{1,0},{2,1},{3,2},{4,3},{5,4},{6,5},{7,6},{8,7},{9,8},{10,9},{11,1... | collective-permute-start | bytes 110600 | tf_op jit(solution)/shard_map/ppermute | solution.py:23
  265.3 1.1 fusion.43
  267.2 1.9 collective-permute-start.12
  270.0 4.9 %collective-permute-done.12 = f32[12,4096]{1,0:T(8,128)S(1)} collective-permute-done((f32[12,4096]{1,0:T(8,128)S(1)}, f32[12,4096]{1,0:T(8,128)S(1)}, u32[]{:S(2)}, u32[]{:S(2)}) %collective-permute-start.12) | collective-permute-done | bytes 196640 | tf_op jit(solution)/shard_map/ppermute | solution.py:33
  274.9 1.0 fusion.45
  (151 shorter events, 16.4 us)
Async XLA Ops:
  0.6 80.2 %copy-start = (bf16[64,64,256]{2,1,0:T(8,128)(2,1)S(1)}, bf16[64,64,256]{2,1,0:T(8,128)(2,1)}, u32[]{:S(2)}) copy-start(bf16[64,64,256]{2,1,0:T(8,128)(2,1)} %param.9) | copy-start | bytes 6291460
  0.6 43.6 %copy-start.8 = (f32[1,1,12,256]{3,1,2,0:T(1,128)S(1)}, f32[1,1,12,256]{3,1,2,0:T(1,128)}, u32[]{:S(2)}) copy-start(f32[1,1,12,256]{3,1,2,0:T(1,128)} %param.14) | copy-start | bytes 36868
  2.8 19.3 %collective-permute-start = (f32[1,1,12,4]{2,3,1,0:T(4,128)S(1)}, f32[1,1,12,4]{2,3,1,0:T(4,128)S(1)}, u32[]{:S(2)}, u32[]{:S(2)}) collective-permute-start(f32[1,1,12,4]{2,3,1,0:T(4,128)S(1)} %maximum_bitcast_fusion), channel_id=1, source_target_pairs={{0,32},{32,64},{64,96},{96,128},{128,160},{160,192},{192,224},{1,3... | collective-permute-start | bytes 584 | tf_op jit(solution)/shard_map/ppermute | solution.py:21
  6.0 16.1 %collective-permute-start.1 = (f32[1,1,12,4]{2,3,1,0:T(4,128)S(1)}, f32[1,1,12,4]{2,3,1,0:T(4,128)S(1)}, u32[]{:S(2)}, u32[]{:S(2)}) collective-permute-start(f32[1,1,12,4]{2,3,1,0:T(4,128)S(1)} %maximum_bitcast_fusion), channel_id=1, source_target_pairs={{32,0},{64,32},{96,64},{128,96},{160,128},{192,160},{224,192},{33,... | collective-permute-start | bytes 584 | tf_op jit(solution)/shard_map/ppermute | solution.py:23
  9.1 56.0 %collective-permute-start.4 = (f32[1,1,12,4096]{3,1,2,0:T(1,128)S(1)}, f32[1,1,12,4096]{3,1,2,0:T(1,128)S(1)}, u32[]{:S(2)}, u32[]{:S(2)}) collective-permute-start(f32[1,1,12,4096]{3,1,2,0:T(1,128)S(1)} %broadcast_multiply_fusion.1), channel_id=1, source_target_pairs={{0,32},{32,64},{64,96},{96,128},{128,160},{160,192},{192,224},{1,3... | collective-permute-start | bytes 589832 | tf_op jit(solution)/shard_map/ppermute | solution.py:21
  12.8 52.4 %collective-permute-start.5 = (f32[1,1,12,4096]{3,1,2,0:T(1,128)S(1)}, f32[1,1,12,4096]{3,1,2,0:T(1,128)S(1)}, u32[]{:S(2)}, u32[]{:S(2)}) collective-permute-start(f32[1,1,12,4096]{3,1,2,0:T(1,128)S(1)} %broadcast_multiply_fusion.1), channel_id=1, source_target_pairs={{32,0},{64,32},{96,64},{128,96},{160,128},{192,160},{224,192},{33,... | collective-permute-start | bytes 589832 | tf_op jit(solution)/shard_map/ppermute | solution.py:23
  14.7 29.6 %collective-permute-start.8 = (f32[1,1,12,256]{3,1,2,0:T(1,128)}, f32[1,1,12,256]{3,1,2,0:T(1,128)S(1)}, u32[]{:S(2)}, u32[]{:S(2)}) collective-permute-start(f32[1,1,12,256]{3,1,2,0:T(1,128)} %param.14), channel_id=1, source_target_pairs={{0,32},{32,64},{64,96},{96,128},{128,160},{160,192},{192,224},{1,3... | collective-permute-start | bytes 36872 | tf_op jit(solution)/shard_map/ppermute | solution.py:21
  22.2 14.6 %collective-permute-start.2 = (f32[3,1,12,4]{2,3,1,0:T(4,128)S(1)}, f32[3,1,12,4]{2,3,1,0:T(4,128)S(1)}, u32[]{:S(2)}, u32[]{:S(2)}) collective-permute-start(f32[3,1,12,4]{2,3,1,0:T(4,128)S(1)} %pad_maximum_fusion.10), channel_id=1, source_target_pairs={{0,1},{1,2},{2,3},{3,4},{4,5},{5,6},{6,7},{7,8},{8,9},{9,10},{10,1... | collective-permute-start | bytes 1736 | tf_op jit(solution)/shard_map/ppermute | solution.py:21
  25.4 13.3 %collective-permute-start.3 = (f32[3,1,12,4]{2,3,1,0:T(4,128)S(1)}, f32[3,1,12,4]{2,3,1,0:T(4,128)S(1)}, u32[]{:S(2)}, u32[]{:S(2)}) collective-permute-start(f32[3,1,12,4]{2,3,1,0:T(4,128)S(1)} %pad_maximum_fusion.10), channel_id=1, source_target_pairs={{1,0},{2,1},{3,2},{4,3},{5,4},{6,5},{7,6},{8,7},{9,8},{10,9},{11,1... | collective-permute-start | bytes 1736 | tf_op jit(solution)/shard_map/ppermute | solution.py:23
  36.8 7.5 %collective-permute-start.9 = (f32[1,1,12,256]{3,1,2,0:T(1,128)}, f32[1,1,12,256]{3,1,2,0:T(1,128)S(1)}, u32[]{:S(2)}, u32[]{:S(2)}) collective-permute-start(f32[1,1,12,256]{3,1,2,0:T(1,128)} %param.14), channel_id=1, source_target_pairs={{32,0},{64,32},{96,64},{128,96},{160,128},{192,160},{224,192},{33,... | collective-permute-start | bytes 36872 | tf_op jit(solution)/shard_map/ppermute | solution.py:23
  44.2 20.2 %copy-start.10 = (f32[2,256]{1,0:T(2,128)S(1)}, f32[2,256]{1,0:T(2,128)}, u32[]{:S(2)}) copy-start(f32[2,256]{1,0:T(2,128)} %param.16) | copy-start | bytes 6148
  44.3 18.8 %collective-permute-start.10 = (f32[3,1,12,256]{3,1,2,0:T(1,128)S(1)}, f32[3,1,12,256]{3,1,2,0:T(1,128)S(1)}, u32[]{:S(2)}, u32[]{:S(2)}) collective-permute-start(f32[3,1,12,256]{3,1,2,0:T(1,128)S(1)} %constant_dynamic-update-slice_fusion), channel_id=1, source_target_pairs={{0,1},{1,2},{2,3},{3,4},{4,5},{5,6},{6,7},{7,8},{8,9},{9,10},{10,1... | collective-permute-start | bytes 110600 | tf_op jit(solution)/shard_map/ppermute | solution.py:21
  49.9 31.7 %copy-start.15 = (f32[48]{0:T(128)}, f32[48]{0:T(128)S(1)}, u32[]{:S(2)}) copy-start(f32[48]{0:T(128)S(1)} %mul.126) | copy-start | bytes 580
  51.7 28.3 %collective-permute-start.15 = (f32[3,1,12,256]{3,1,2,0:T(1,128)S(1)}, f32[3,1,12,256]{3,1,2,0:T(1,128)S(1)}, u32[]{:S(2)}, u32[]{:S(2)}) collective-permute-start(f32[3,1,12,256]{3,1,2,0:T(1,128)S(1)} %constant_dynamic-update-slice_fusion), channel_id=1, source_target_pairs={{1,0},{2,1},{3,2},{4,3},{5,4},{6,5},{7,6},{8,7},{9,8},{10,9},{11,1... | collective-permute-start | bytes 110600 | tf_op jit(solution)/shard_map/ppermute | solution.py:23
  66.6 25.2 %collective-permute-start.6 = (f32[3,1,12,4096]{3,1,2,0:T(1,128)}, f32[3,1,12,4096]{3,1,2,0:T(1,128)}, u32[]{:S(2)}, u32[]{:S(2)}) collective-permute-start(f32[3,1,12,4096]{3,1,2,0:T(1,128)} %pad_maximum_fusion.1), channel_id=1, source_target_pairs={{0,1},{1,2},{2,3},{3,4},{4,5},{5,6},{6,7},{7,8},{8,9},{9,10},{10,1... | collective-permute-start | bytes 1769480 | tf_op jit(solution)/shard_map/ppermute | solution.py:21
  68.5 24.9 %collective-permute-start.7 = (f32[3,1,12,4096]{3,1,2,0:T(1,128)}, f32[3,1,12,4096]{3,1,2,0:T(1,128)}, u32[]{:S(2)}, u32[]{:S(2)}) collective-permute-start(f32[3,1,12,4096]{3,1,2,0:T(1,128)} %pad_maximum_fusion.1), channel_id=1, source_target_pairs={{1,0},{2,1},{3,2},{4,3},{5,4},{6,5},{7,6},{8,7},{9,8},{10,9},{11,1... | collective-permute-start | bytes 1769480 | tf_op jit(solution)/shard_map/ppermute | solution.py:23
  98.8 4.0 %copy-start.7 = (s32[108,64]{1,0:T(8,128)S(1)}, s32[108,64]{1,0:T(8,128)}, u32[]{:S(2)}) copy-start(s32[108,64]{1,0:T(8,128)} %iota_add_fusion.3) | copy-start | bytes 82948
  131.7 15.9 %copy-start.16 = (f32[48]{0:T(128)S(1)}, f32[48]{0:T(128)}, u32[]{:S(2)}) copy-start(f32[48]{0:T(128)} %copy-done.15) | copy-start | bytes 580
  131.7 15.9 %copy-start.18 = (f32[48]{0:T(128)S(1)}, f32[48]{0:T(128)}, u32[]{:S(2)}) copy-start(f32[48]{0:T(128)} %reshape.345) | copy-start | bytes 580
  131.7 15.9 %copy-start.21 = (f32[48]{0:T(128)S(1)}, f32[48]{0:T(128)}, u32[]{:S(2)}) copy-start(f32[48]{0:T(128)} %compare_select_fusion.1) | copy-start | bytes 580
  133.1 14.5 %copy-start.1 = (f32[48,4096]{1,0:T(8,128)S(1)}, f32[48,4096]{1,0:T(8,128)}, u32[]{:S(2)}) copy-start(f32[48,4096]{1,0:T(8,128)} %reshape.330) | copy-start | bytes 2359300
  134.9 15.0 %copy-start.4 = (f32[48,4096]{1,0:T(8,128)S(1)}, f32[48,4096]{1,0:T(8,128)}, u32[]{:S(2)}) copy-start(f32[48,4096]{1,0:T(8,128)} %mul.125) | copy-start | bytes 2359300
  134.9 15.0 %copy-start.5 = (f32[48,4096]{1,0:T(8,128)S(1)}, f32[48,4096]{1,0:T(8,128)}, u32[]{:S(2)}) copy-start(f32[48,4096]{1,0:T(8,128)} %convolution_subtract_fusion.4) | copy-start | bytes 2359300
  134.9 15.0 %copy-start.20 = (f32[48]{0:T(128)S(1)}, f32[48]{0:T(128)}, u32[]{:S(2)}) copy-start(f32[48]{0:T(128)} %reshape.344) | copy-start | bytes 580
  135.0 18.6 %collective-permute-start.13 = (f32[2,12,256]{2,1,0:T(8,128)S(1)}, f32[2,12,256]{2,1,0:T(8,128)S(1)}, u32[]{:S(2)}, u32[]{:S(2)}) collective-permute-start(f32[2,12,256]{2,1,0:T(8,128)S(1)} %slice_bitcast_fusion.4), channel_id=1, source_target_pairs={{1,0},{2,1},{3,2},{4,3},{5,4},{6,5},{7,6},{8,7},{9,8},{10,9},{11,1... | collective-permute-start | bytes 73736 | tf_op jit(solution)/shard_map/ppermute | solution.py:33
  150.0 1.0 copy-start.19
  150.9 19.9 %copy-start.6 = (f32[108,256]{1,0:T(8,128)S(1)}, f32[108,256]{1,0:T(8,128)}, u32[]{:S(2)}) copy-start(f32[108,256]{1,0:T(8,128)} %reshape.338) | copy-start | bytes 331780
  150.9 19.9 %copy-start.9 = (f32[1,1,12,256]{3,1,2,0:T(1,128)S(1)}, f32[1,1,12,256]{3,1,2,0:T(1,128)}, u32[]{:S(2)}) copy-start(f32[1,1,12,256]{3,1,2,0:T(1,128)} %param.14) | copy-start | bytes 36868
  151.0 19.9 %copy-start.14 = (pred[12]{0:T(512)(128)(4,1)S(1)}, pred[12]{0:T(512)(128)(4,1)}, u32[]{:S(2)}) copy-start(pred[12]{0:T(512)(128)(4,1)} %get-tuple-element.23) | copy-start | bytes 40
  151.0 24.5 %copy-start.17 = (f32[48]{0:T(128)S(1)}, f32[48]{0:T(128)}, u32[]{:S(2)}) copy-start(f32[48]{0:T(128)} %reshape.342) | copy-start | bytes 580
  153.6 17.3 %collective-permute-start.14 = (f32[12,256]{1,0:T(8,128)S(1)}, f32[12,256]{1,0:T(8,128)S(1)}, u32[]{:S(2)}, u32[]{:S(2)}) collective-permute-start(f32[12,256]{1,0:T(8,128)S(1)} %slice_bitcast_fusion.6), channel_id=1, source_target_pairs={{32,0},{64,32},{96,64},{128,96},{160,128},{192,160},{224,192},{33,... | collective-permute-start | bytes 36872 | tf_op jit(solution)/shard_map/ppermute | solution.py:33
  171.1 11.0 %collective-permute-start.16 = (f32[1,1,12,256]{3,2,1,0:T(8,128)S(1)}, f32[1,1,12,256]{3,2,1,0:T(8,128)S(1)}, u32[]{:S(2)}, u32[]{:S(2)}) collective-permute-start(f32[1,1,12,256]{3,2,1,0:T(8,128)S(1)} %bitcast.136), channel_id=1, source_target_pairs={{0,32},{32,64},{64,96},{96,128},{128,160},{160,192},{192,224},{1,3... | collective-permute-start | bytes 36872 | tf_op jit(solution)/shard_map/ppermute | solution.py:21
  173.0 9.1 %collective-permute-start.17 = (f32[1,1,12,256]{3,2,1,0:T(8,128)S(1)}, f32[1,1,12,256]{3,2,1,0:T(8,128)S(1)}, u32[]{:S(2)}, u32[]{:S(2)}) collective-permute-start(f32[1,1,12,256]{3,2,1,0:T(8,128)S(1)} %bitcast.137), channel_id=1, source_target_pairs={{32,0},{64,32},{96,64},{128,96},{160,128},{192,160},{224,192},{33,... | collective-permute-start | bytes 36872 | tf_op jit(solution)/shard_map/ppermute | solution.py:23
  179.1 16.4 %copy-start.3 = (pred[2,2,12,64,64]{3,4,2,1,0:T(32,128)(4,1)S(1)}, pred[2,2,12,64,64]{3,4,2,1,0:T(32,128)(4,1)}, u32[]{:S(2)}) copy-start(pred[2,2,12,64,64]{3,4,2,1,0:T(32,128)(4,1)} %add_compare_fusion.1) | copy-start | bytes 589828
  182.1 17.1 %copy-start.13 = (pred[12]{0:T(512)(128)(4,1)S(1)}, pred[12]{0:T(512)(128)(4,1)}, u32[]{:S(2)}) copy-start(pred[12]{0:T(512)(128)(4,1)} %get-tuple-element.24) | copy-start | bytes 40
  182.1 17.0 %collective-permute-start.18 = (f32[3,1,12,256]{3,2,1,0:T(8,128)S(1)}, f32[3,1,12,256]{3,2,1,0:T(8,128)S(1)}, u32[]{:S(2)}, u32[]{:S(2)}) collective-permute-start(f32[3,1,12,256]{3,2,1,0:T(8,128)S(1)} %pad_maximum_fusion.7), channel_id=1, source_target_pairs={{0,1},{1,2},{2,3},{3,4},{4,5},{5,6},{6,7},{7,8},{8,9},{9,10},{10,1... | collective-permute-start | bytes 110600 | tf_op jit(solution)/shard_map/ppermute | solution.py:21
  184.1 15.1 %collective-permute-start.19 = (f32[3,1,12,256]{3,2,1,0:T(8,128)S(1)}, f32[3,1,12,256]{3,2,1,0:T(8,128)S(1)}, u32[]{:S(2)}, u32[]{:S(2)}) collective-permute-start(f32[3,1,12,256]{3,2,1,0:T(8,128)S(1)} %pad_maximum_fusion.7), channel_id=1, source_target_pairs={{1,0},{2,1},{3,2},{4,3},{5,4},{6,5},{7,6},{8,7},{9,8},{10,9},{11,1... | collective-permute-start | bytes 110600 | tf_op jit(solution)/shard_map/ppermute | solution.py:23
  199.4 11.2 %collective-permute-start.20 = (f32[1,1,12,256]{3,2,1,0:T(8,128)S(1)}, f32[1,1,12,256]{3,2,1,0:T(8,128)S(1)}, u32[]{:S(2)}, u32[]{:S(2)}) collective-permute-start(f32[1,1,12,256]{3,2,1,0:T(8,128)S(1)} %bitcast.140), channel_id=1, source_target_pairs={{0,32},{32,64},{64,96},{96,128},{128,160},{160,192},{192,224},{1,3... | collective-permute-start | bytes 36872 | tf_op jit(solution)/shard_map/ppermute | solution.py:21
  203.1 7.5 %collective-permute-start.21 = (f32[1,1,12,256]{3,2,1,0:T(8,128)S(1)}, f32[1,1,12,256]{3,2,1,0:T(8,128)S(1)}, u32[]{:S(2)}, u32[]{:S(2)}) collective-permute-start(f32[1,1,12,256]{3,2,1,0:T(8,128)S(1)} %bitcast.141), channel_id=1, source_target_pairs={{32,0},{64,32},{96,64},{128,96},{160,128},{192,160},{224,192},{33,... | collective-permute-start | bytes 36872 | tf_op jit(solution)/shard_map/ppermute | solution.py:23
  208.7 18.9 %copy-start.12 = (pred[12]{0:T(512)(128)(4,1)S(1)}, pred[12]{0:T(512)(128)(4,1)}, u32[]{:S(2)}) copy-start(pred[12]{0:T(512)(128)(4,1)} %get-tuple-element.22) | copy-start | bytes 40
  210.6 58.5 %copy-start.11 = (pred[12]{0:T(512)(128)(4,1)S(1)}, pred[12]{0:T(512)(128)(4,1)}, u32[]{:S(2)}) copy-start(pred[12]{0:T(512)(128)(4,1)} %get-tuple-element.21) | copy-start | bytes 40
  210.6 16.8 %collective-permute-start.22 = (f32[3,1,12,256]{3,2,1,0:T(8,128)S(1)}, f32[3,1,12,256]{3,2,1,0:T(8,128)S(1)}, u32[]{:S(2)}, u32[]{:S(2)}) collective-permute-start(f32[3,1,12,256]{3,2,1,0:T(8,128)S(1)} %pad_maximum_fusion.8), channel_id=1, source_target_pairs={{0,1},{1,2},{2,3},{3,4},{4,5},{5,6},{6,7},{7,8},{8,9},{9,10},{10,1... | collective-permute-start | bytes 110600 | tf_op jit(solution)/shard_map/ppermute | solution.py:21
  212.6 14.9 %collective-permute-start.23 = (f32[3,1,12,256]{3,2,1,0:T(8,128)S(1)}, f32[3,1,12,256]{3,2,1,0:T(8,128)S(1)}, u32[]{:S(2)}, u32[]{:S(2)}) collective-permute-start(f32[3,1,12,256]{3,2,1,0:T(8,128)S(1)} %pad_maximum_fusion.8), channel_id=1, source_target_pairs={{1,0},{2,1},{3,2},{4,3},{5,4},{6,5},{7,6},{8,7},{9,8},{10,9},{11,1... | collective-permute-start | bytes 110600 | tf_op jit(solution)/shard_map/ppermute | solution.py:23
  224.9 40.4 %collective-permute-start.11 = (f32[2,12,4096]{2,1,0:T(8,128)}, f32[2,12,4096]{2,1,0:T(8,128)}, u32[]{:S(2)}, u32[]{:S(2)}) collective-permute-start(f32[2,12,4096]{2,1,0:T(8,128)} %slice_bitcast_fusion), channel_id=1, source_target_pairs={{1,0},{2,1},{3,2},{4,3},{5,4},{6,5},{7,6},{8,7},{9,8},{10,9},{11,1... | collective-permute-start | bytes 1179656 | tf_op jit(solution)/shard_map/ppermute | solution.py:33
  227.7 10.3 %collective-permute-start.24 = (f32[1,1,12,256]{3,2,1,0:T(8,128)S(1)}, f32[1,1,12,256]{3,2,1,0:T(8,128)S(1)}, u32[]{:S(2)}, u32[]{:S(2)}) collective-permute-start(f32[1,1,12,256]{3,2,1,0:T(8,128)S(1)} %bitcast.132), channel_id=1, source_target_pairs={{0,32},{32,64},{64,96},{96,128},{128,160},{160,192},{192,224},{1,3... | collective-permute-start | bytes 36872 | tf_op jit(solution)/shard_map/ppermute | solution.py:21
  232.2 19.6 %collective-permute-start.25 = (f32[1,1,12,256]{3,2,1,0:T(8,128)S(1)}, f32[1,1,12,256]{3,2,1,0:T(8,128)S(1)}, u32[]{:S(2)}, u32[]{:S(2)}) collective-permute-start(f32[1,1,12,256]{3,2,1,0:T(8,128)S(1)} %bitcast.133), channel_id=1, source_target_pairs={{32,0},{64,32},{96,64},{128,96},{160,128},{192,160},{224,192},{33,... | collective-permute-start | bytes 36872 | tf_op jit(solution)/shard_map/ppermute | solution.py:23
  251.8 17.3 %collective-permute-start.26 = (f32[3,1,12,256]{3,2,1,0:T(8,128)S(1)}, f32[3,1,12,256]{3,2,1,0:T(8,128)S(1)}, u32[]{:S(2)}, u32[]{:S(2)}) collective-permute-start(f32[3,1,12,256]{3,2,1,0:T(8,128)S(1)} %pad_maximum_fusion.9), channel_id=1, source_target_pairs={{0,1},{1,2},{2,3},{3,4},{4,5},{5,6},{6,7},{7,8},{8,9},{9,10},{10,1... | collective-permute-start | bytes 110600 | tf_op jit(solution)/shard_map/ppermute | solution.py:21
  253.8 15.4 %collective-permute-start.27 = (f32[3,1,12,256]{3,2,1,0:T(8,128)S(1)}, f32[3,1,12,256]{3,2,1,0:T(8,128)S(1)}, u32[]{:S(2)}, u32[]{:S(2)}) collective-permute-start(f32[3,1,12,256]{3,2,1,0:T(8,128)S(1)} %pad_maximum_fusion.9), channel_id=1, source_target_pairs={{1,0},{2,1},{3,2},{4,3},{5,4},{6,5},{7,6},{8,7},{9,8},{10,9},{11,1... | collective-permute-start | bytes 110600 | tf_op jit(solution)/shard_map/ppermute | solution.py:23
  266.4 0.8 copy-start.2
  267.2 7.7 %collective-permute-start.12 = (f32[12,4096]{1,0:T(8,128)S(1)}, f32[12,4096]{1,0:T(8,128)S(1)}, u32[]{:S(2)}, u32[]{:S(2)}) collective-permute-start(f32[12,4096]{1,0:T(8,128)S(1)} %slice_bitcast_fusion.2), channel_id=1, source_target_pairs={{32,0},{64,32},{96,64},{128,96},{160,128},{192,160},{224,192},{33,... | collective-permute-start | bytes 589832 | tf_op jit(solution)/shard_map/ppermute | solution.py:33
where the time goes:
time: 278 us; the launch traced here: 277 us
  starting transfers between devices  133 us (48%)
  waiting for transfers between devices  47.6 us (17%)
  matrix products  45.5 us (16%)
  local copies, waits for them, and re-layouts  30.8 us (11%)
  other arithmetic  17.4 us (6%)
    ppermute x12, starting transfers between devices, padded(): lax.ppermute(head, axis, [((i + 1) % count, i) for i in range(ends)])  79.6 us
    ppermute x12, starting transfers between devices, padded(): lax.ppermute(tail, axis, [(i, (i + 1) % count) for i in range(ends)])  33.4 us
    ppermute x4, starting transfers between devices, shifted(): lax.ppermute(value, axis, [(source, source + steps) for source in range(i...  19.8 us
    ppermute x4, waiting for transfers between devices, shifted(): lax.ppermute(value, axis, [(source, source + steps) for source in range(i...  19.5 us
    ppermute x12, waiting for transfers between devices, padded(): lax.ppermute(head, axis, [((i + 1) % count, i) for i in range(ends)])  15.5 us
    ppermute x12, waiting for transfers between devices, padded(): lax.ppermute(tail, axis, [(i, (i + 1) % count) for i in range(ends)])  12.7 us
    dot_general x1, matrix products, on_device(): coupling = jnp.dot(owned, flattened.T, precision=exact_mode)  8.99 us
    dot_general x4, matrix products, on_device(): coupled = jnp.dot(intersection_time, values, precision=exact_mode)  8.78 us
  transfers between devices with their start and end apart: 28, of which 6 were waited for; matrix products, arithmetic and copies ran while one was open for 17% of the time, Pallas kernels for 0%

commit v1 on v0

v1 whole, which is shorter than its diff:
```python
import functools

import jax
import jax.numpy as jnp
from jax import lax
from jax.experimental import pallas as pl
from jax.experimental.pallas import tpu as pltpu
from jax.sharding import PartitionSpec as P

MESH = pl.DeviceIdType.MESH
F32 = jnp.float32
BF16 = jnp.bfloat16
I32 = jnp.int32
I16 = jnp.int16

SIDE = 64
PIX = SIDE * SIDE
FRAMES = 256
SLOTS = 12
GROUPS = 4
PAD = 16
NEAR = 4 * PAD
BIG = 1e30
TOP = 8.0

DIRS = ((-1, -1), (-1, 0), (-1, 1), (0, -1), (0, 1), (1, -1), (1, 0), (1, 1))
UL, UP, UR, LEFT, RIGHT, DL, DOWN, DR = range(8)
OWN = 8
TILE_SETS = (
    (UL, UP, LEFT, OWN),
    (UP, UR, OWN, RIGHT),
    (LEFT, OWN, DL, DOWN),
    (OWN, RIGHT, DOWN, DR),
)
SELF_AT = (3, 2, 1, 0)


def nt(a, b):
    return lax.dot_general(a, b, (((1,), (1,)), ((), ())), preferred_element_type=F32)


def mm(a, b):
    return jnp.dot(a, b, preferred_element_type=F32)


def split(x):
    high = x.astype(BF16)
    return high, (x - high.astype(F32)).astype(BF16)


def turn(x, shift, forward):
    for bit in range(12):
        step = 1 << bit
        chosen = ((shift >> bit) & 1) == 1
        by = step if forward else PIX - step
        if by % 128 == 0:
            moved = jnp.concatenate([x[:, PIX - by :], x[:, : PIX - by]], axis=1)
        else:
            moved = pltpu.roll(x, by, 1)
        x = jnp.where(chosen, moved, x)
    return x


def half_turn(x, forward):
    return pltpu.roll(x, SIDE if forward else PIX - SIDE, 1)


def kernel(
    rows, cols,
    anchors, groups, counts, window,
    footprints, temporal, back, back_time, movie_hbm,
    out_shapes, out_traces,
    movie, pad_f, hl, code, r_code, cm, r_cm, near_cm, target, canvas, x3,
    shares, share_out, r_share, wave, r_wave, call_f, c_high, c_low, temp,
    piece_up, r_piece, merged, r_merged,
    movie_sem, cm_send, cm_recv, r_send, r_recv, s_send, s_recv, t_send, t_recv, p_send, p_recv, m_send, m_recv,
):
    r = lax.axis_index("row")
    c = lax.axis_index("col")

    def there(d):
        down, right = DIRS[d]
        ok = None
        for at, step, count in ((r, down, rows), (c, right, cols)):
            if step:
                one = at + step >= 0 if step < 0 else at + step < count
                ok = one if ok is None else ok & one
        return ok

    def place(d):
        return (r + DIRS[d][0], c + DIRS[d][1])

    barrier = pltpu.get_barrier_semaphore()

    r_cm[...] = jnp.zeros_like(r_cm)
    r_share[...] = jnp.zeros_like(r_share)
    r_wave[...] = jnp.zeros_like(r_wave)

    expected = 0
    for d in range(8):
        ok = there(d)

        @pl.when(ok)
        def _(d=d):
            pl.semaphore_signal(barrier, inc=1, device_id=place(d), device_id_type=MESH)

        expected = expected + ok.astype(I32)

    load_movie = pltpu.make_async_copy(movie_hbm, movie, movie_sem)
    load_movie.start()

    sub = lax.broadcasted_iota(I32, (PAD, 128), 0)
    lane = lax.broadcasted_iota(I32, (PAD, 128), 1)
    g_sub = jnp.full((PAD, 128), -1, I32)
    g_lane = jnp.full((PAD, 128), -1, I32)
    a_lane = jnp.zeros((PAD, 128), I32)
    b_lane = jnp.zeros((PAD, 128), I32)
    count = counts[0, 0]
    for m in range(SLOTS):
        g_sub = jnp.where(sub == m, groups[0, 0, m], g_sub)
        g_lane = jnp.where(lane == m, groups[0, 0, m], g_lane)
        a_lane = jnp.where(lane == m, anchors[0, 0, m, 0], a_lane)
        b_lane = jnp.where(lane == m, anchors[0, 0, m, 1], b_lane)
    alive_lane = lane < count
    alive_sub = sub < count
    a_lane = jnp.where(alive_lane, a_lane, 0)
    b_lane = jnp.where(alive_lane, b_lane, 0)
    same = g_sub == g_lane
    before_lane = jnp.sum(jnp.where(same & (sub < lane), 1.0, 0.0), axis=0, keepdims=True)
    before_sub = jnp.sum(jnp.where(same & (lane < sub), 1.0, 0.0), axis=1, keepdims=True)
    pos_lane = g_lane.astype(F32) * 4.0 + before_lane
    pos_sub = g_sub.astype(F32) * 4.0 + before_sub
    pick = jnp.where((sub.astype(F32) == pos_lane) & (lane < SLOTS), 1.0, 0.0)
    unpick = jnp.where((lane.astype(F32) == pos_sub) & (sub < SLOTS), 1.0, 0.0)
    a_own = jnp.sum(pick * a_lane.astype(F32), axis=1, keepdims=True)
    b_own = jnp.sum(pick * b_lane.astype(F32), axis=1, keepdims=True)
    live_own = jnp.sum(pick * jnp.where(alive_lane, 1.0, 0.0), axis=1, keepdims=True)
    shift_own = (a_own * float(SIDE) + b_own).astype(I32)
    pick16 = pick[:, :PAD]
    unpick16 = unpick[:, :PAD]

    pad_f[SLOTS:PAD, :] = jnp.zeros((PAD - SLOTS, PIX), F32)
    pad_f[:SLOTS, :FRAMES] = temporal[...]
    cm[:, :FRAMES] = jnp.dot(pick16, pad_f[:, :FRAMES], precision=lax.Precision.HIGHEST, preferred_element_type=F32)
    cm[:, FRAMES:] = jnp.where(lane == 0, a_own, jnp.where(lane == 1, b_own, jnp.where(lane == 2, live_own, 0.0)))

    pad_f[:SLOTS, :] = footprints[...]
    whole = jnp.floor(pad_f[...] * 65535.0 + 0.5)
    upper = jnp.floor(whole * (1.0 / 256.0))
    hl[:PAD, :] = upper.astype(BF16)
    hl[PAD:, :] = (whole - upper * 256.0).astype(BF16)
    pick_hl = jnp.concatenate([pick16 * 256.0, pick16], axis=1).astype(BF16)
    pad_f[...] = mm(pick_hl, hl[...])
    for half in range(2):
        part = slice(half * 8, half * 8 + 8)
        pad_f[part, :] = turn(pad_f[part, :], shift_own[part], True)
    code[...] = (pad_f[...] - 32768.0).astype(I32).astype(I16)

    pl.semaphore_wait(barrier, expected)

    def remote(src, dst, send, recv, d):
        return pltpu.make_async_remote_copy(
            src_ref=src, dst_ref=dst, send_sem=send, recv_sem=recv, device_id=place(d), device_id_type=MESH
        )

    pending = []

    def start(copy, ok):
        @pl.when(ok)
        def _():
            copy.start()

        pending.append((copy, ok))

    def arrived(copy, ok):
        @pl.when(ok)
        def _():
            copy.wait_recv()

    def cm_copy(src, slot, d):
        return remote(src, r_cm.at[slot], cm_send.at[slot], cm_recv.at[slot], d)

    for d in (RIGHT, LEFT, DOWN, UP):
        start(cm_copy(cm, 7 - d, d), there(d))
    start(remote(code, r_code.at[2], r_send.at[2], r_recv.at[2], RIGHT), there(RIGHT))
    start(remote(code, r_code.at[1], r_send.at[1], r_recv.at[1], DOWN), there(DOWN))

    arrived(cm_copy(cm, LEFT, LEFT), there(LEFT))
    start(cm_copy(r_cm.at[LEFT], DL, UP), there(UP) & there(LEFT))
    start(cm_copy(r_cm.at[LEFT], UL, DOWN), there(DOWN) & there(LEFT))
    arrived(cm_copy(cm, RIGHT, RIGHT), there(RIGHT))
    start(cm_copy(r_cm.at[RIGHT], DR, UP), there(UP) & there(RIGHT))
    start(cm_copy(r_cm.at[RIGHT], UR, DOWN), there(DOWN) & there(RIGHT))
    for d in (UP, UL, DOWN, UR, DL, DR):
        arrived(cm_copy(cm, d, d), there(d))

    def cm_of(tile, rows_at, lanes_at):
        if tile == OWN:
            return cm[rows_at, lanes_at]
        return r_cm[tile, rows_at, lanes_at]

    for g in range(GROUPS):
        for t in range(4):
            at = slice(g * PAD + t * 4, g * PAD + t * 4 + 4)
            near_cm[at, :] = cm_of(TILE_SETS[0][t], slice(g * 4, g * 4 + 4), slice(None))
    for k in range(4):
        for g in range(GROUPS):
            for t in range(4):
                at = slice(k * NEAR + g * PAD + t * 4, k * NEAR + g * PAD + t * 4 + 4)
                call_f[at, :] = cm_of(TILE_SETS[k][t], slice(g * 4, g * 4 + 4), slice(0, FRAMES))
    high, low = split(call_f[...])
    c_high[...] = high
    c_low[...] = low

    frame = lax.broadcasted_iota(I32, (NEAR, FRAMES), 1)
    weighted = jnp.where((frame >= window[0]) & (frame < window[1]), near_cm[:, :FRAMES], 0.0)
    w_high, w_low = split(weighted)
    w_both = jnp.concatenate([w_high, w_low], axis=0)
    q4 = nt(w_both, w_both)
    q = q4[:NEAR, :NEAR] + q4[:NEAR, NEAR:] + q4[NEAR:, :NEAR] + q4[NEAR:, NEAR:]
    a_near = near_cm[:, FRAMES : FRAMES + 1].astype(I32)
    b_near = near_cm[:, FRAMES + 1 : FRAMES + 2].astype(I32)
    live_near = near_cm[:, FRAMES + 2 : FRAMES + 3]
    eye = lax.broadcasted_iota(I32, (NEAR, NEAR), 0) == lax.broadcasted_iota(I32, (NEAR, NEAR), 1)
    mass = jnp.sum(jnp.where(eye, q, 0.0), axis=1, keepdims=True)
    inverse = 1.0 / jnp.where(live_near > 0, mass, 1.0)
    q_high, q_low = split(jnp.where(eye, 0.0, q) * inverse)
    q3 = jnp.concatenate([q_high, q_high, q_low], axis=1)
    load0 = jnp.sum(weighted * back_time[0:1, :], axis=1, keepdims=True)
    load1 = jnp.sum(weighted * back_time[1:2, :], axis=1, keepdims=True)

    tile_at = (lax.broadcasted_iota(I32, (NEAR, 1), 0) >> 2) & 3
    above = tile_at < 2
    aside = (tile_at & 1) == 0
    y_low = jnp.where(above, 0, a_near)
    y_high = jnp.where(live_near > 0, jnp.where(above, a_near, SIDE), 0)
    x_low = jnp.where(aside, 0, b_near)
    x_high = jnp.where(aside, b_near, SIDE)

    def covered(rows_at, begin, width):
        spot = lax.broadcasted_iota(I32, (1, width), 1) + begin
        y = spot >> 6
        x = spot & 63
        return (
            (y >= y_low[rows_at]) & (y < y_high[rows_at]) & (x >= x_low[rows_at]) & (x < x_high[rows_at])
        )

    load_movie.wait()
    width = 1024
    for begin in range(0, PIX, width):
        at = slice(begin, begin + width)
        pull = nt(w_high, movie[at, :])
        pull = pull - load0 * back[0:1, at].astype(F32) - load1 * back[1:2, at].astype(F32)
        target[:, at] = jnp.where(covered(slice(None), begin, width), pull * inverse, -BIG)

    arrived(remote(code, r_code.at[2], r_send.at[2], r_recv.at[2], LEFT), there(LEFT))
    start(remote(r_code.at[2], r_code.at[0], r_send.at[0], r_recv.at[0], DOWN), there(DOWN) & there(LEFT))
    arrived(remote(code, r_code.at[1], r_send.at[1], r_recv.at[1], UP), there(UP))
    arrived(remote(code, r_code.at[0], r_send.at[0], r_recv.at[0], UL), there(UL))
    for t in (0, 1, 2, 3):
        coded = (r_code[t] if t < 3 else code[...]).astype(I32).astype(F32)
        if t in (0, 2):
            coded = half_turn(coded, False)
        for g in range(GROUPS):
            canvas[g * PAD + t * 4 : g * PAD + t * 4 + 4, :] = coded[g * 4 : g * 4 + 4, :]
    for g in range(GROUPS):
        rows_at = slice(g * PAD, g * PAD + PAD)
        value = jnp.where(covered(rows_at, 0, PIX), (canvas[rows_at, :] + 32768.0) * (1.0 / 65535.0), 0.0)
        high, low = split(value)
        x3[g * PAD : g * PAD + PAD, :] = high
        x3[NEAR + g * PAD : NEAR + g * PAD + PAD, :] = low
        x3[2 * NEAR + g * PAD : 2 * NEAR + g * PAD + PAD, :] = high

    both = x3[: 2 * NEAR, :]
    gram = nt(both, both)
    overlap = gram[:NEAR, :NEAR] + gram[:NEAR, NEAR:] + gram[NEAR:, :NEAR] + gram[NEAR:, NEAR:]
    loading = nt(both, back[...])
    loading = loading[:NEAR] + loading[NEAR:]
    drive = mm(x3[:NEAR, :], movie[...])
    drive = drive - loading[:, 0:1] * back_time[0:1, :] - loading[:, 1:2] * back_time[1:2, :]
    shares[:, :FRAMES] = drive
    shares[:, FRAMES : FRAMES + NEAR] = overlap
    shares[:, FRAMES + NEAR :] = jnp.zeros((NEAR, 128 - NEAR), F32)
    for t in range(4):
        for g in range(GROUPS):
            share_out[t, g * 4 : g * 4 + 4, :] = shares[g * PAD + t * 4 : g * PAD + t * 4 + 4, :]

    def share_copy(t, d):
        return remote(share_out.at[t], r_share.at[t], s_send.at[t], s_recv.at[t], d)

    for t, d in ((0, UL), (2, LEFT), (1, UP)):
        start(share_copy(t, d), there(d))

    for g in range(GROUPS):
        rows_at = slice(g * PAD, g * PAD + PAD)
        value = jnp.maximum(target[rows_at, :] - mm(q3[rows_at, :], x3[...]), 0.0)
        canvas[rows_at, :] = jnp.floor(jnp.sqrt(value * (1.0 / TOP)) * 65535.0 + 0.5) - 32768.0
        if g < GROUPS - 1:
            high, low = split(value)
            x3[g * PAD : g * PAD + PAD, :] = high
            x3[NEAR + g * PAD : NEAR + g * PAD + PAD, :] = low
            x3[2 * NEAR + g * PAD : 2 * NEAR + g * PAD + PAD, :] = high

    def gather_tile(t):
        for g in range(GROUPS):
            temp[g * 4 : g * 4 + 4, :] = canvas[g * PAD + t * 4 : g * PAD + t * 4 + 4, :]
        return temp[...]

    for t in range(2):
        piece_up[t] = gather_tile(t).astype(I32).astype(I16)

    def piece_copy(t, d):
        return remote(piece_up.at[t], r_piece.at[t], p_send.at[t], p_recv.at[t], d)

    for t in range(2):
        start(piece_copy(t, UP), there(UP))

    for t, d in ((2, RIGHT), (1, DOWN), (0, DR)):
        arrived(share_copy(t, d), there(d))
    parts = [share_out[3], r_share[2], r_share[1], r_share[0]]
    drive = parts[0][:, :FRAMES] + parts[1][:, :FRAMES] + parts[2][:, :FRAMES] + parts[3][:, :FRAMES]
    near_lane = lax.broadcasted_iota(I32, (PAD, NEAR), 1)
    near_row = lax.broadcasted_iota(I32, (PAD, NEAR), 0)
    lane_row = ((near_lane >> 4) << 2) + (near_lane & 3)
    lane_tile = (near_lane >> 2) & 3
    weight = jnp.zeros((PAD, 1), F32)
    others = []
    for k in range(4):
        v = parts[k][:, FRAMES : FRAMES + NEAR]
        mine = (lane_tile == SELF_AT[k]) & (lane_row == near_row)
        weight = weight + jnp.sum(jnp.where(mine, v, 0.0), axis=1, keepdims=True)
        others.append(jnp.where(mine, 0.0, v))
    scale = 1.0 / jnp.where(live_own > 0, weight, 1.0)
    v_high, v_low = split(jnp.concatenate(others, axis=1) * scale)
    v_both = jnp.concatenate([v_high, v_low], axis=0)
    goal = drive * scale
    own = cm[:, :FRAMES]
    row_group = lax.broadcasted_iota(I32, (PAD, FRAMES), 0) >> 2

    def wave_copy(g, d, slot):
        return remote(wave.at[g], r_wave.at[g, slot], t_send.at[g, slot], t_recv.at[g, slot], d)

    for g in range(GROUPS):
        if g > 0:
            for d in range(8):
                arrived(wave_copy(g - 1, d, d), there(d))
            for k in range(4):
                for t in range(4):
                    tile = TILE_SETS[k][t]
                    new = wave[g - 1] if tile == OWN else r_wave[g - 1, tile]
                    at = slice(k * NEAR + (g - 1) * PAD + t * 4, k * NEAR + (g - 1) * PAD + t * 4 + 4)
                    call_f[at, :128] = new[:4, :]
                    call_f[at, 128:] = new[4:, :]
                at = slice(k * NEAR + (g - 1) * PAD, k * NEAR + g * PAD)
                high, low = split(call_f[at, :])
                c_high[at, :] = high
                c_low[at, :] = low
        product = mm(v_both, c_high[...])
        coupled = product[:PAD] + product[PAD:] + mm(v_high, c_low[...])
        chosen = (row_group == g) & (live_own > 0)
        own = jnp.where(chosen, jnp.maximum(goal - coupled, 0.0), own)
        if g < GROUPS - 1:
            wave[g, :4, :] = own[g * 4 : g * 4 + 4, :128]
            wave[g, 4:, :] = own[g * 4 : g * 4 + 4, 128:]
            for d in (UR, DR, UL, DL, RIGHT, LEFT, UP, DOWN):
                start(wave_copy(g, d, 7 - d), there(d))
        if g == 0:
            for t in range(2):
                arrived(piece_copy(t, DOWN), there(DOWN))
            spot = lax.broadcasted_iota(I32, (PAD, PIX), 1)
            a_left = r_cm[LEFT, :, FRAMES : FRAMES + 1].astype(I32)
            below = (spot >> 6) < a_left
            merged[...] = jnp.where(below, r_piece[0].astype(I32), gather_tile(2).astype(I32)).astype(I16)
            start(remote(merged, r_merged, m_send, m_recv, LEFT), there(LEFT))

    back_own = jnp.dot(unpick16, own, precision=lax.Precision.HIGHEST, preferred_element_type=F32)
    out_traces[...] = jnp.where(alive_sub[:SLOTS, 0:1], back_own[:SLOTS, :], temporal[...])

    arrived(remote(merged, r_merged, m_send, m_recv, RIGHT), there(RIGHT))
    y = spot >> 6
    x = spot & 63
    a_int = a_own.astype(I32)
    b_int = b_own.astype(I32)
    far = half_turn(r_merged[...].astype(I32).astype(F32), True)
    near = jnp.where(y < a_int, r_piece[1].astype(I32).astype(F32), gather_tile(3))
    pad_f[...] = jnp.where(x < b_int, far, near) + 32768.0
    for half in range(2):
        part = slice(half * 8, half * 8 + 8)
        pad_f[part, :] = turn(pad_f[part, :], shift_own[part], False)
    whole = pad_f[...]
    upper = jnp.floor(whole * (1.0 / 256.0))
    hl[:PAD, :] = upper.astype(BF16)
    hl[PAD:, :] = (whole - upper * 256.0).astype(BF16)
    unpick_hl = jnp.concatenate([unpick16 * 256.0, unpick16], axis=1).astype(BF16)
    root = mm(unpick_hl, hl[...])[:SLOTS, :] * (1.0 / 65535.0)
    out_shapes[...] = root * root * TOP

    for copy, ok in pending:
        @pl.when(ok)
        def _(copy=copy):
            copy.wait_send()


def on_device(rows, cols, movie, footprints, anchors, groups, counts, temporal, back_spatial, back_temporal, window):
    vmem = pl.BlockSpec(memory_space=pltpu.VMEM)
    smem = pl.BlockSpec(memory_space=pltpu.SMEM)
    dma = pltpu.SemaphoreType.DMA
    shapes, traces = pl.pallas_call(
        functools.partial(kernel, rows, cols),
        out_shape=(
            jax.ShapeDtypeStruct((SLOTS, PIX), F32),
            jax.ShapeDtypeStruct((SLOTS, FRAMES), F32),
        ),
        in_specs=[smem] * 4 + [vmem] * 4 + [pl.BlockSpec(memory_space=pl.ANY)],
        out_specs=(vmem, vmem),
        scratch_shapes=[
            pltpu.VMEM((PIX, FRAMES), BF16),
            pltpu.VMEM((PAD, PIX), F32),
            pltpu.VMEM((2 * PAD, PIX), BF16),
            pltpu.VMEM((PAD, PIX), I16),
            pltpu.VMEM((3, PAD, PIX), I16),
            pltpu.VMEM((PAD, FRAMES + 128), F32),
            pltpu.VMEM((8, PAD, FRAMES + 128), F32),
            pltpu.VMEM((NEAR, FRAMES + 128), F32),
            pltpu.VMEM((NEAR, PIX), F32),
            pltpu.VMEM((NEAR, PIX), F32),
            pltpu.VMEM((3 * NEAR, PIX), BF16),
            pltpu.VMEM((NEAR, FRAMES + 128), F32),
            pltpu.VMEM((4, PAD, FRAMES + 128), F32),
            pltpu.VMEM((3, PAD, FRAMES + 128), F32),
            pltpu.VMEM((3, 8, 128), F32),
            pltpu.VMEM((3, 8, 8, 128), F32),
            pltpu.VMEM((4 * NEAR, FRAMES), F32),
            pltpu.VMEM((4 * NEAR, FRAMES), BF16),
            pltpu.VMEM((4 * NEAR, FRAMES), BF16),
            pltpu.VMEM((PAD, PIX), F32),
            pltpu.VMEM((2, PAD, PIX), I16),
            pltpu.VMEM((2, PAD, PIX), I16),
            pltpu.VMEM((PAD, PIX), I16),
            pltpu.VMEM((PAD, PIX), I16),
            dma,
            dma((8,)),
            dma((8,)),
            dma((3,)),
            dma((3,)),
            dma((3,)),
            dma((3,)),
            dma((3, 8)),
            dma((3, 8)),
            dma((2,)),
            dma((2,)),
            dma,
            dma,
        ],
        compiler_params=pltpu.CompilerParams(collective_id=0, has_side_effects=True, vmem_limit_bytes=48 << 20),
    )(
        anchors,
        groups,
        counts,
        window,
        footprints.reshape(SLOTS, PIX),
        temporal.reshape(SLOTS, FRAMES),
        back_spatial.reshape(2, PIX),
        back_temporal,
        movie.reshape(PIX, FRAMES),
    )
    return shapes[None, None], traces[None, None]


def solution(mesh):
    return jax.shard_map(
        functools.partial(on_device, mesh.shape["row"], mesh.shape["col"]),
        mesh=mesh,
        in_specs=(
            P("row", "col", None),
            P("row", "col", None, None),
            P("row", "col", None, None),
            P("row", "col", None),
            P("row", "col"),
            P("row", "col", None, None),
            P(None, "row", "col"),
            P(),
            P(),
        ),
        out_specs=(P("row", "col", None, None), P("row", "col", None, None)),
        check_vma=False,
    )
```

time: 278 us -> 66.4 us (0.24)
  the two profiles are of different devices: /device:TPU:129 before, /device:TPU:192 now
where the time goes in v1:
time: 66.4 us; the launch traced here: 66.1 us
  Pallas kernels  56.3 us (85%)
  local copies, waits for them, and re-layouts  8.45 us (13%)
  between operations  1.3 us (2%)
    pallas_call x1, Pallas kernels, on_device(): pl.pallas_call(functools.partial(kernel, rows, cols), out_shape=(jax.Shap...  56.3 us
    unnamed x13, local copies, waits for them, and re-layouts  7.59 us

profile of v1, /device:TPU:192, one launch (start us, length us, event | category | flops | bytes accessed | tf_op | source)
XLA Modules:
  0.0 66.1 jit_solution(6153964182911573244)
XLA Ops:
  1.3 0.8 %copy.11.anchors = s32[1,1,12,2]{3,2,1,0:T(8,128)S(1)} copy(s32[1,1,12,2]{2,3,1,0:T(2,128)} %param.11) | data formatting | bytes 192 | tf_op args[2]
  2.0 0.7 %copy.19 = f32[1,1,12,256]{3,2,1,0:T(8,128)S(1)} copy(f32[1,1,12,256]{3,1,2,0:T(1,128)} %param.14) | data formatting | bytes 24576
  2.8 0.9 %reshape.18.back = bf16[2,4096]{1,0:T(2,128)(2,1)S(1)} reshape(bf16[2,64,64]{2,1,0:T(8,128)(2,1)} %param.15) | data formatting | bytes 32768 | tf_op jit(solution)/shard_map/reshape | solution.py:463
  3.6 1.0 %copy.18 = f32[1,1,12,4096]{3,2,1,0:T(8,128)S(1)} copy(f32[1,1,12,4096]{3,1,2,0:T(1,128)} %param.10) | data formatting | bytes 393216
  4.7 0.0 copy-start
  4.7 1.6 %copy-done = bf16[64,64,256]{2,1,0:T(8,128)(2,1)S(1)} copy-done((bf16[64,64,256]{2,1,0:T(8,128)(2,1)S(1)}, bf16[64,64,256]{2,1,0:T(8,128)(2,1)}, u32[]{:S(2)}) %copy-start) | copy-done | bytes 2097176
  6.3 0.0 copy-start.1
  6.3 0.7 %copy-done.1 = f32[2,256]{1,0:T(2,128)S(1)} copy-done((f32[2,256]{1,0:T(2,128)S(1)}, f32[2,256]{1,0:T(2,128)}, u32[]{:S(2)}) %copy-start.1) | copy-done | bytes 2072
  6.9 0.0 copy-start.2
  6.9 0.7 copy-done.2
  7.6 0.0 copy-start.3
  7.6 0.7 copy-done.3
  8.2 56.3 %shard_map.104 = (f32[12,4096]{1,0:T(8,128)S(1)}, f32[12,256]{1,0:T(8,128)S(1)}) custom-call(s32[1,1,12,2]{3,2,1,0:T(8,128)S(1)} %copy.11.anchors, s32[1,1,12]{2,1,0:T(1,128)S(1)} %copy-done.2, s32[1,1]{1,0:T(1,128)S(6)} %copy.20.counts, s32[2]{0:T(128)S(1)} %copy-done.3, f32[12,4096]{1,0:T(8,128)S(1)} %bitcast.10, f32[12,256]{1,0:T(8,128)S(1)} %bitcast.12, ...), custom_call_target="tpu_custom_call" | custom-call | tf_op jit(solution)/shard_map/pallas_call | solution.py:408
  64.6 0.9 %copy.12 = f32[1,1,12,4096]{3,1,2,0:T(1,128)} copy(f32[1,1,12,4096]{3,2,1,0:T(8,128)S(1)} %bitcast.11) | data formatting | bytes 393216
  65.5 0.6 copy.13
Async XLA Ops:
  4.7 1.6 %copy-start = (bf16[64,64,256]{2,1,0:T(8,128)(2,1)S(1)}, bf16[64,64,256]{2,1,0:T(8,128)(2,1)}, u32[]{:S(2)}) copy-start(bf16[64,64,256]{2,1,0:T(8,128)(2,1)} %param.9) | copy-start | bytes 6291460
  6.3 0.7 %copy-start.1 = (f32[2,256]{1,0:T(2,128)S(1)}, f32[2,256]{1,0:T(2,128)}, u32[]{:S(2)}) copy-start(f32[2,256]{1,0:T(2,128)} %back_time.1) | copy-start | bytes 6148
  6.9 0.7 copy-start.2
  7.6 0.7 copy-start.3

commit v2 on v1

--- a/solution.py
+++ b/solution.py
@@ -67,13 +67,12 @@
 
 def kernel(
     rows, cols,
-    anchors, groups, counts, window,
-    footprints, temporal, back, back_time, movie_hbm,
+    anchors_in, groups_in, counts_in, window_in, footprints_in, temporal_in, back_in, back_time_in, movie_in,
     out_shapes, out_traces,
-    movie, pad_f, hl, code, r_code, cm, r_cm, near_cm, target, canvas, x3,
+    anchors, groups, counts, window, footprints, temporal, back_raw, back_time, movie, back_even, back, pad_f, hl, code, r_code, cm, r_cm, near_cm, target, canvas, x3,
     shares, share_out, r_share, wave, r_wave, call_f, c_high, c_low, temp,
     piece_up, r_piece, merged, r_merged,
-    movie_sem, cm_send, cm_recv, r_send, r_recv, s_send, s_recv, t_send, t_recv, p_send, p_recv, m_send, m_recv,
+    load_sem, cm_send, cm_recv, r_send, r_recv, s_send, s_recv, t_send, t_recv, p_send, p_recv, m_send, m_recv,
 ):
     r = lax.axis_index("row")
     c = lax.axis_index("col")
@@ -92,6 +91,25 @@
 
     barrier = pltpu.get_barrier_semaphore()
 
+    loads = [
+        pltpu.make_async_copy(source, target_ref, load_sem.at[at])
+        for at, (source, target_ref) in enumerate(
+            (
+                (groups_in, groups),
+                (anchors_in, anchors),
+                (counts_in, counts),
+                (window_in, window),
+                (temporal_in, temporal),
+                (footprints_in, footprints),
+                (back_time_in, back_time),
+                (back_in, back_raw),
+                (movie_in, movie),
+            )
+        )
+    ]
+    for load in loads:
+        load.start()
+
     r_cm[...] = jnp.zeros_like(r_cm)
     r_share[...] = jnp.zeros_like(r_share)
     r_wave[...] = jnp.zeros_like(r_wave)
@@ -106,9 +124,8 @@
 
         expected = expected + ok.astype(I32)
 
-    load_movie = pltpu.make_async_copy(movie_hbm, movie, movie_sem)
-    load_movie.start()
-
+    for load in loads[:5]:
+        load.wait()
     sub = lax.broadcasted_iota(I32, (PAD, 128), 0)
     lane = lax.broadcasted_iota(I32, (PAD, 128), 1)
     g_sub = jnp.full((PAD, 128), -1, I32)
@@ -117,10 +134,10 @@
     b_lane = jnp.zeros((PAD, 128), I32)
     count = counts[0, 0]
     for m in range(SLOTS):
-        g_sub = jnp.where(sub == m, groups[0, 0, m], g_sub)
-        g_lane = jnp.where(lane == m, groups[0, 0, m], g_lane)
-        a_lane = jnp.where(lane == m, anchors[0, 0, m, 0], a_lane)
-        b_lane = jnp.where(lane == m, anchors[0, 0, m, 1], b_lane)
+        g_sub = jnp.where(sub == m, groups[0, m], g_sub)
+        g_lane = jnp.where(lane == m, groups[0, m], g_lane)
+        a_lane = jnp.where(lane == m, anchors[0, m], a_lane)
+        b_lane = jnp.where(lane == m, anchors[1, m], b_lane)
     alive_lane = lane < count
     alive_sub = sub < count
     a_lane = jnp.where(alive_lane, a_lane, 0)
@@ -140,11 +157,15 @@
     unpick16 = unpick[:, :PAD]
 
     pad_f[SLOTS:PAD, :] = jnp.zeros((PAD - SLOTS, PIX), F32)
-    pad_f[:SLOTS, :FRAMES] = temporal[...]
+    for half in range(2):
+        pad_f[:SLOTS, half * 128 : half * 128 + 128] = temporal[pl.ds(half, SLOTS, stride=2), :]
+    old_traces = pad_f[:SLOTS, :FRAMES]
     cm[:, :FRAMES] = jnp.dot(pick16, pad_f[:, :FRAMES], precision=lax.Precision.HIGHEST, preferred_element_type=F32)
     cm[:, FRAMES:] = jnp.where(lane == 0, a_own, jnp.where(lane == 1, b_own, jnp.where(lane == 2, live_own, 0.0)))
 
-    pad_f[:SLOTS, :] = footprints[...]
+    loads[5].wait()
+    for q in range(PIX // 128):
+        pad_f[:SLOTS, q * 128 : q * 128 + 128] = footprints[pl.ds(q, SLOTS, stride=32), :]
     whole = jnp.floor(pad_f[...] * 65535.0 + 0.5)
     upper = jnp.floor(whole * (1.0 / 256.0))
     hl[:PAD, :] = upper.astype(BF16)
@@ -155,6 +176,17 @@
         part = slice(half * 8, half * 8 + 8)
         pad_f[part, :] = turn(pad_f[part, :], shift_own[part], True)
     code[...] = (pad_f[...] - 32768.0).astype(I32).astype(I16)
+
+    loads[6].wait()
+    loads[7].wait()
+    for i in range(2):
+        back_even[i * SIDE : i * SIDE + SIDE, :SIDE] = back_raw[i].astype(F32)
+    even = back_even[pl.ds(0, SIDE, stride=2), :SIDE]
+    odd = back_even[pl.ds(1, SIDE, stride=2), :SIDE]
+    back_even[:SIDE, :] = jnp.concatenate([even, odd], axis=1)
+    for q in range(PIX // 128):
+        back[:2, q * 128 : q * 128 + 128] = back_even[pl.ds(q, 2, stride=32), :]
+    back[2:, :] = jnp.zeros((6, PIX), F32)
 
     pl.semaphore_wait(barrier, expected)
 
@@ -245,12 +277,12 @@
             (y >= y_low[rows_at]) & (y < y_high[rows_at]) & (x >= x_low[rows_at]) & (x < x_high[rows_at])
         )
 
-    load_movie.wait()
+    loads[8].wait()
     width = 1024
     for begin in range(0, PIX, width):
         at = slice(begin, begin + width)
         pull = nt(w_high, movie[at, :])
-        pull = pull - load0 * back[0:1, at].astype(F32) - load1 * back[1:2, at].astype(F32)
+        pull = pull - load0 * back[0:1, at] - load1 * back[1:2, at]
         target[:, at] = jnp.where(covered(slice(None), begin, width), pull * inverse, -BIG)
 
     arrived(remote(code, r_code.at[2], r_send.at[2], r_recv.at[2], LEFT), there(LEFT))
@@ -274,7 +306,7 @@
     both = x3[: 2 * NEAR, :]
     gram = nt(both, both)
     overlap = gram[:NEAR, :NEAR] + gram[:NEAR, NEAR:] + gram[NEAR:, :NEAR] + gram[NEAR:, NEAR:]
-    loading = nt(both, back[...])
+    loading = nt(both, back[...].astype(BF16))
     loading = loading[:NEAR] + loading[NEAR:]
     drive = mm(x3[:NEAR, :], movie[...])
     drive = drive - loading[:, 0:1] * back_time[0:1, :] - loading[:, 1:2] * back_time[1:2, :]
@@ -374,7 +406,9 @@
             start(remote(merged, r_merged, m_send, m_recv, LEFT), there(LEFT))
 
     back_own = jnp.dot(unpick16, own, precision=lax.Precision.HIGHEST, preferred_element_type=F32)
-    out_traces[...] = jnp.where(alive_sub[:SLOTS, 0:1], back_own[:SLOTS, :], temporal[...])
+    new_traces = jnp.where(alive_sub[:SLOTS, 0:1], back_own[:SLOTS, :], old_traces)
+    for half in range(2):
+        out_traces[pl.ds(half, SLOTS, stride=2), :] = new_traces[:, half * 128 : half * 128 + 128]
 
     arrived(remote(merged, r_merged, m_send, m_recv, RIGHT), there(RIGHT))
     y = spot >> 6
@@ -393,7 +427,9 @@
     hl[PAD:, :] = (whole - upper * 256.0).astype(BF16)
     unpick_hl = jnp.concatenate([unpick16 * 256.0, unpick16], axis=1).astype(BF16)
     root = mm(unpick_hl, hl[...])[:SLOTS, :] * (1.0 / 65535.0)
-    out_shapes[...] = root * root * TOP
+    pad_f[:SLOTS, :] = root * root * TOP
+    for q in range(PIX // 128):
+        out_shapes[pl.ds(q, SLOTS, stride=32), :] = pad_f[:SLOTS, q * 128 : q * 128 + 128]
 
     for copy, ok in pending:
         @pl.when(ok)
@@ -403,18 +439,27 @@
 
 def on_device(rows, cols, movie, footprints, anchors, groups, counts, temporal, back_spatial, back_temporal, window):
     vmem = pl.BlockSpec(memory_space=pltpu.VMEM)
-    smem = pl.BlockSpec(memory_space=pltpu.SMEM)
     dma = pltpu.SemaphoreType.DMA
     shapes, traces = pl.pallas_call(
         functools.partial(kernel, rows, cols),
         out_shape=(
-            jax.ShapeDtypeStruct((SLOTS, PIX), F32),
-            jax.ShapeDtypeStruct((SLOTS, FRAMES), F32),
+            jax.ShapeDtypeStruct((SLOTS * PIX // 128, 128), F32),
+            jax.ShapeDtypeStruct((SLOTS * FRAMES // 128, 128), F32),
         ),
-        in_specs=[smem] * 4 + [vmem] * 4 + [pl.BlockSpec(memory_space=pl.ANY)],
+        in_specs=[pl.BlockSpec(memory_space=pl.ANY)] * 9,
         out_specs=(vmem, vmem),
         scratch_shapes=[
+            pltpu.SMEM((2, SLOTS), I32),
+            pltpu.SMEM((1, SLOTS), I32),
+            pltpu.SMEM((1, 1), I32),
+            pltpu.SMEM((2,), I32),
+            pltpu.VMEM((SLOTS * PIX // 128, 128), F32),
+            pltpu.VMEM((SLOTS * FRAMES // 128, 128), F32),
+            pltpu.VMEM((2, SIDE, SIDE), BF16),
+            pltpu.VMEM((2, FRAMES), F32),
             pltpu.VMEM((PIX, FRAMES), BF16),
+            pltpu.VMEM((2 * SIDE, 2 * SIDE), F32),
+            pltpu.VMEM((8, PIX), F32),
             pltpu.VMEM((PAD, PIX), F32),
             pltpu.VMEM((2 * PAD, PIX), BF16),
             pltpu.VMEM((PAD, PIX), I16),
@@ -438,7 +483,7 @@
             pltpu.VMEM((2, PAD, PIX), I16),
             pltpu.VMEM((PAD, PIX), I16),
             pltpu.VMEM((PAD, PIX), I16),
-            dma,
+            dma((9,)),
             dma((8,)),
             dma((8,)),
             dma((3,)),
@@ -452,19 +497,19 @@
             dma,
             dma,
         ],
-        compiler_params=pltpu.CompilerParams(collective_id=0, has_side_effects=True, vmem_limit_bytes=48 << 20),
+        compiler_params=pltpu.CompilerParams(collective_id=0, has_side_effects=True),
     )(
-        anchors,
-        groups,
+        anchors.reshape(SLOTS, 2).T,
+        groups.reshape(1, SLOTS),
         counts,
         window,
-        footprints.reshape(SLOTS, PIX),
-        temporal.reshape(SLOTS, FRAMES),
-        back_spatial.reshape(2, PIX),
+        footprints.reshape(SLOTS * PIX // 128, 128),
+        temporal.reshape(SLOTS * FRAMES // 128, 128),
+        back_spatial,
         back_temporal,
         movie.reshape(PIX, FRAMES),
     )
-    return shapes[None, None], traces[None, None]
+    return shapes.reshape(1, 1, SLOTS, PIX), traces.reshape(1, 1, SLOTS, FRAMES)
 
 
 def solution(mesh):

time: 66.4 us -> 61 us (0.919)
  local copies, waits for them, and re-layouts: 8.45 us -> 2.92 us
    unnamed x13 -> x2, local copies, waits for them, and re-layouts: 7.59 us -> 2.92 us
    reshape x1 -> x0, local copies, waits for them, and re-layouts: 0.85 us -> none  [on_device(): back_spatial.reshape(2, PIX)]
where the time goes in v2:
time: 61 us; the launch traced here: 60.9 us
  Pallas kernels  56.7 us (93%)
  local copies, waits for them, and re-layouts  2.92 us (5%)
  between operations  1.29 us (2%)
    pallas_call x1, Pallas kernels, on_device(): pl.pallas_call(functools.partial(kernel, rows, cols), out_shape=(jax.Shap...  56.7 us
    unnamed x2, local copies, waits for them, and re-layouts  2.92 us

profile of v2, /device:TPU:192, one launch (start us, length us, event | category | flops | bytes accessed | tf_op | source)
XLA Modules:
  0.0 60.9 jit_solution(7085706035172303594)
XLA Ops:
  1.3 56.7 %shard_map.104 = (f32[384,128]{1,0:T(8,128)}, f32[24,128]{1,0:T(8,128)}) custom-call(s32[2,12]{1,0:T(2,128)} %bitcast.14, s32[1,12]{1,0:T(1,128)} %bitcast.15, s32[1,1]{1,0:T(1,128)S(6)} %copy.17.counts_in, s32[2]{0:T(128)} %window_in.1, f32[384,128]{1,0:T(8,128)} %bitcast.10, f32[24,128]{1,0:T(8,128)} %bitcast.12, bf16[2,64,64]{2,1,0:T(8,128)(2,1)} %back_in.1, ...), custom_call_target="tpu_custom_call" | custom-call | tf_op jit(solution)/shard_map/pallas_call | solution.py:443
  57.9 1.6 %copy.18 = f32[1,1,12,4096]{3,1,2,0:T(1,128)} copy(f32[1,1,12,4096]{3,1,2,0:T(1,128)} %bitcast.11) | data formatting | bytes 393216
  59.6 1.3 %copy.19 = f32[1,1,12,256]{3,1,2,0:T(1,128)} copy(f32[1,1,12,256]{3,1,2,0:T(1,128)} %bitcast.13) | data formatting | bytes 24576

commit v3 on v2

--- a/solution.py
+++ b/solution.py
@@ -32,7 +32,7 @@
     (LEFT, OWN, DL, DOWN),
     (OWN, RIGHT, DOWN, DR),
 )
-SELF_AT = (3, 2, 1, 0)
+HALVES = 2
 
 
 def nt(a, b):
@@ -67,12 +67,14 @@
 
 def kernel(
     rows, cols,
-    anchors_in, groups_in, counts_in, window_in, footprints_in, temporal_in, back_in, back_time_in, movie_in,
+    counts, anchors_in, groups_in, window_in, footprints_in, temporal_in, back_in, back_time_in, movie_in,
     out_shapes, out_traces,
-    anchors, groups, counts, window, footprints, temporal, back_raw, back_time, movie, back_even, back, pad_f, hl, code, r_code, cm, r_cm, near_cm, target, canvas, x3,
+    anchors, groups, window, footprints, temporal, back_raw, back_time, movie, back_even, back, pad_f, hl, code, r_code, cm, r_cm, near_cm, target, canvas, x3,
     shares, share_out, r_share, wave, r_wave, call_f, c_high, c_low, temp,
+    r_mate, mate_cm, mate_goal, mate_v, mate_wave, r_far, mate_f, mate_high, mate_low,
     piece_up, r_piece, merged, r_merged,
     load_sem, cm_send, cm_recv, r_send, r_recv, s_send, s_recv, t_send, t_recv, p_send, p_recv, m_send, m_recv,
+    mate_send, mate_recv, mw_send, far_send, far_recv,
 ):
     r = lax.axis_index("row")
     c = lax.axis_index("col")
@@ -89,6 +91,14 @@
     def place(d):
         return (r + DIRS[d][0], c + DIRS[d][1])
 
+    west = c == cols // 2 - 1
+    east = c == cols // 2
+    beside_west = c == cols // 2 - 2
+    beside_east = c == cols // 2 + 1
+
+    def row_ok(step):
+        return (r + step >= 0) & (r + step < rows)
+
     barrier = pltpu.get_barrier_semaphore()
 
     loads = [
@@ -97,7 +107,6 @@
             (
                 (groups_in, groups),
                 (anchors_in, anchors),
-                (counts_in, counts),
                 (window_in, window),
                 (temporal_in, temporal),
                 (footprints_in, footprints),
@@ -113,6 +122,14 @@
     r_cm[...] = jnp.zeros_like(r_cm)
     r_share[...] = jnp.zeros_like(r_share)
     r_wave[...] = jnp.zeros_like(r_wave)
+    r_mate[...] = jnp.zeros_like(r_mate)
+    r_far[...] = jnp.zeros_like(r_far)
+    call_f[...] = jnp.zeros_like(call_f)
+    c_high[...] = jnp.zeros_like(c_high)
+    c_low[...] = jnp.zeros_like(c_low)
+    mate_f[...] = jnp.zeros_like(mate_f)
+    mate_high[...] = jnp.zeros_like(mate_high)
+    mate_low[...] = jnp.zeros_like(mate_low)
 
     expected = 0
     for d in range(8):
@@ -123,8 +140,17 @@
             pl.semaphore_signal(barrier, inc=1, device_id=place(d), device_id_type=MESH)
 
         expected = expected + ok.astype(I32)
-
-    for load in loads[:5]:
+    for down in (-1, 0, 1):
+        for right, role in ((2, beside_west | west), (-2, beside_east | east)):
+            ok = role & row_ok(down)
+
+            @pl.when(ok)
+            def _(down=down, right=right):
+                pl.semaphore_signal(barrier, inc=1, device_id=(r + down, c + right), device_id_type=MESH)
+
+            expected = expected + ok.astype(I32)
+
+    for load in loads[:4]:
         load.wait()
     sub = lax.broadcasted_iota(I32, (PAD, 128), 0)
     lane = lax.broadcasted_iota(I32, (PAD, 128), 1)
@@ -163,7 +189,7 @@
     cm[:, :FRAMES] = jnp.dot(pick16, pad_f[:, :FRAMES], precision=lax.Precision.HIGHEST, preferred_element_type=F32)
     cm[:, FRAMES:] = jnp.where(lane == 0, a_own, jnp.where(lane == 1, b_own, jnp.where(lane == 2, live_own, 0.0)))
 
-    loads[5].wait()
+    loads[4].wait()
     for q in range(PIX // 128):
         pad_f[:SLOTS, q * 128 : q * 128 + 128] = footprints[pl.ds(q, SLOTS, stride=32), :]
     whole = jnp.floor(pad_f[...] * 65535.0 + 0.5)
@@ -177,8 +203,8 @@
         pad_f[part, :] = turn(pad_f[part, :], shift_own[part], True)
     code[...] = (pad_f[...] - 32768.0).astype(I32).astype(I16)
 
+    loads[5].wait()
     loads[6].wait()
-    loads[7].wait()
     for i in range(2):
         back_even[i * SIDE : i * SIDE + SIDE, :SIDE] = back_raw[i].astype(F32)
     even = back_even[pl.ds(0, SIDE, stride=2), :SIDE]
@@ -191,8 +217,9 @@
     pl.semaphore_wait(barrier, expected)
 
     def remote(src, dst, send, recv, d):
+        target_id = place(d) if isinstance(d, int) else (r + d[0], c + d[1])
         return pltpu.make_async_remote_copy(
-            src_ref=src, dst_ref=dst, send_sem=send, recv_sem=recv, device_id=place(d), device_id_type=MESH
+            src_ref=src, dst_ref=dst, send_sem=send, recv_sem=recv, device_id=target_id, device_id_type=MESH
         )
 
     pending = []
@@ -214,8 +241,16 @@
 
     for d in (RIGHT, LEFT, DOWN, UP):
         start(cm_copy(cm, 7 - d, d), there(d))
-    start(remote(code, r_code.at[2], r_send.at[2], r_recv.at[2], RIGHT), there(RIGHT))
-    start(remote(code, r_code.at[1], r_send.at[1], r_recv.at[1], DOWN), there(DOWN))
+
+    def code_copy(source, slot, part, d):
+        at = pl.ds(part * (PIX // HALVES), PIX // HALVES)
+        source = code.at[:, at] if source is None else r_code.at[source, :, at]
+        return remote(source, r_code.at[slot, :, at], r_send.at[slot, part], r_recv.at[slot, part], d)
+
+    for part in range(HALVES):
+        start(code_copy(None, 2, part, RIGHT), there(RIGHT))
+    for part in range(HALVES):
+        start(code_copy(None, 1, part, DOWN), there(DOWN))
 
     arrived(cm_copy(cm, LEFT, LEFT), there(LEFT))
     start(cm_copy(r_cm.at[LEFT], DL, UP), there(UP) & there(LEFT))
@@ -235,14 +270,7 @@
         for t in range(4):
             at = slice(g * PAD + t * 4, g * PAD + t * 4 + 4)
             near_cm[at, :] = cm_of(TILE_SETS[0][t], slice(g * 4, g * 4 + 4), slice(None))
-    for k in range(4):
-        for g in range(GROUPS):
-            for t in range(4):
-                at = slice(k * NEAR + g * PAD + t * 4, k * NEAR + g * PAD + t * 4 + 4)
-                call_f[at, :] = cm_of(TILE_SETS[k][t], slice(g * 4, g * 4 + 4), slice(0, FRAMES))
-    high, low = split(call_f[...])
-    c_high[...] = high
-    c_low[...] = low
+    near_high, near_low = split(near_cm[:, :FRAMES])
 
     frame = lax.broadcasted_iota(I32, (NEAR, FRAMES), 1)
     weighted = jnp.where((frame >= window[0]) & (frame < window[1]), near_cm[:, :FRAMES], 0.0)
@@ -277,7 +305,7 @@
             (y >= y_low[rows_at]) & (y < y_high[rows_at]) & (x >= x_low[rows_at]) & (x < x_high[rows_at])
         )
 
-    loads[8].wait()
+    loads[7].wait()
     width = 1024
     for begin in range(0, PIX, width):
         at = slice(begin, begin + width)
@@ -285,10 +313,13 @@
         pull = pull - load0 * back[0:1, at] - load1 * back[1:2, at]
         target[:, at] = jnp.where(covered(slice(None), begin, width), pull * inverse, -BIG)
 
-    arrived(remote(code, r_code.at[2], r_send.at[2], r_recv.at[2], LEFT), there(LEFT))
-    start(remote(r_code.at[2], r_code.at[0], r_send.at[0], r_recv.at[0], DOWN), there(DOWN) & there(LEFT))
-    arrived(remote(code, r_code.at[1], r_send.at[1], r_recv.at[1], UP), there(UP))
-    arrived(remote(code, r_code.at[0], r_send.at[0], r_recv.at[0], UL), there(UL))
+    for part in range(HALVES):
+        arrived(code_copy(None, 2, part, LEFT), there(LEFT))
+        start(code_copy(2, 0, part, DOWN), there(DOWN) & there(LEFT))
+    for part in range(HALVES):
+        arrived(code_copy(None, 1, part, UP), there(UP))
+    for part in range(HALVES):
+        arrived(code_copy(None, 0, part, UL), there(UL))
     for t in (0, 1, 2, 3):
         coded = (r_code[t] if t < 3 else code[...]).astype(I32).astype(F32)
         if t in (0, 2):
@@ -310,9 +341,13 @@
     loading = loading[:NEAR] + loading[NEAR:]
     drive = mm(x3[:NEAR, :], movie[...])
     drive = drive - loading[:, 0:1] * back_time[0:1, :] - loading[:, 1:2] * back_time[1:2, :]
-    shares[:, :FRAMES] = drive
+    self_overlap = jnp.sum(jnp.where(eye, overlap, 0.0), axis=1, keepdims=True)
+    overlap = jnp.where(eye, 0.0, overlap)
+    o_high, o_low = split(overlap)
+    product = mm(jnp.concatenate([o_high, o_low], axis=0), near_high)
+    shares[:, :FRAMES] = drive - (product[:NEAR] + product[NEAR:] + mm(o_high, near_low))
     shares[:, FRAMES : FRAMES + NEAR] = overlap
-    shares[:, FRAMES + NEAR :] = jnp.zeros((NEAR, 128 - NEAR), F32)
+    shares[:, FRAMES + NEAR :] = jnp.broadcast_to(self_overlap, (NEAR, 128 - NEAR))
     for t in range(4):
         for g in range(GROUPS):
             share_out[t, g * 4 : g * 4 + 4, :] = shares[g * PAD + t * 4 : g * PAD + t * 4 + 4, :]
@@ -322,6 +357,17 @@
 
     for t, d in ((0, UL), (2, LEFT), (1, UP)):
         start(share_copy(t, d), there(d))
+
+    def mate_share(t, k, d):
+        return remote(share_out.at[t], r_mate.at[k], mate_send.at[t], mate_recv.at[k], d)
+
+    start(mate_share(3, 0, (0, 1)), west)
+    start(mate_share(1, 2, (-1, 1)), west & row_ok(-1))
+    start(mate_share(3, 0, (0, -1)), east)
+    start(mate_share(1, 2, (-1, -1)), east & row_ok(-1))
+    start(mate_share(0, 3, (-1, 0)), east & row_ok(-1))
+    start(mate_share(2, 1, (0, -2)), beside_east)
+    start(mate_share(0, 3, (-1, -2)), beside_east & row_ok(-1))
 
     for g in range(GROUPS):
         rows_at = slice(g * PAD, g * PAD + PAD)
@@ -349,53 +395,91 @@
 
     for t, d in ((2, RIGHT), (1, DOWN), (0, DR)):
         arrived(share_copy(t, d), there(d))
-    parts = [share_out[3], r_share[2], r_share[1], r_share[0]]
-    drive = parts[0][:, :FRAMES] + parts[1][:, :FRAMES] + parts[2][:, :FRAMES] + parts[3][:, :FRAMES]
-    near_lane = lax.broadcasted_iota(I32, (PAD, NEAR), 1)
-    near_row = lax.broadcasted_iota(I32, (PAD, NEAR), 0)
-    lane_row = ((near_lane >> 4) << 2) + (near_lane & 3)
-    lane_tile = (near_lane >> 2) & 3
-    weight = jnp.zeros((PAD, 1), F32)
-    others = []
-    for k in range(4):
-        v = parts[k][:, FRAMES : FRAMES + NEAR]
-        mine = (lane_tile == SELF_AT[k]) & (lane_row == near_row)
-        weight = weight + jnp.sum(jnp.where(mine, v, 0.0), axis=1, keepdims=True)
-        others.append(jnp.where(mine, 0.0, v))
-    scale = 1.0 / jnp.where(live_own > 0, weight, 1.0)
-    v_high, v_low = split(jnp.concatenate(others, axis=1) * scale)
-    v_both = jnp.concatenate([v_high, v_low], axis=0)
-    goal = drive * scale
+
+    def joined(parts, live):
+        total = parts[0] + parts[1] + parts[2] + parts[3]
+        scale = 1.0 / jnp.where(live > 0, total[:, FRAMES + NEAR : FRAMES + NEAR + 1], 1.0)
+        v = jnp.concatenate([part[:, FRAMES : FRAMES + NEAR] for part in parts], axis=1) * scale
+        return total[:, :FRAMES] * scale, jnp.concatenate(split(v), axis=0)
+
+    goal, v_both = joined([share_out[3], r_share[2], r_share[1], r_share[0]], live_own)
     own = cm[:, :FRAMES]
     row_group = lax.broadcasted_iota(I32, (PAD, FRAMES), 0) >> 2
 
+    def changes(sources, g, full, high_ref, low_ref):
+        for k in range(4):
+            for t in range(4):
+                new = sources[TILE_SETS[k][t]]
+                at = slice(k * NEAR + g * PAD + t * 4, k * NEAR + g * PAD + t * 4 + 4)
+                full[at, :128] = new[:4, :]
+                full[at, 128:] = new[4:, :]
+            at = slice(k * NEAR + g * PAD, k * NEAR + g * PAD + PAD)
+            high, low = split(full[at, :])
+            high_ref[at, :] = high
+            low_ref[at, :] = low
+
+    def updated(g, aim, v_two, high_ref, low_ref, old, live):
+        left_over = aim
+        if g > 0:
+            product = mm(v_two, high_ref[...])
+            left_over = aim - (product[:PAD] + product[PAD:] + mm(v_two[:PAD], low_ref[...]))
+        chosen = (row_group == g) & (live > 0)
+        return jnp.where(chosen, jnp.maximum(left_over, 0.0), old)
+
+    def pack(ref, g, new, old):
+        change = new - old
+        ref[g, :4, :] = change[g * 4 : g * 4 + 4, :128]
+        ref[g, 4:, :] = change[g * 4 : g * 4 + 4, 128:]
+
     def wave_copy(g, d, slot):
         return remote(wave.at[g], r_wave.at[g, slot], t_send.at[g, slot], t_recv.at[g, slot], d)
+
+    def wave_ok(d):
+        ok = there(d)
+        if DIRS[d][1] > 0:
+            ok = ok & jnp.logical_not(west)
+        if DIRS[d][1] < 0:
+            ok = ok & jnp.logical_not(east)
+        return ok
+
+    def mate_copy(g, at, d, slot):
+        return remote(mate_wave.at[g], r_wave.at[g, slot], mw_send.at[g, at], t_recv.at[g, slot], d)
+
+    def far_copy(g, down, right):
+        return remote(wave.at[g], r_far.at[g, 1 - down], far_send.at[g, 1 - down], far_recv.at[g, 1 - down], (down, right))
+
+    sides = (
+        (west, RIGHT, UR, DR, {UL: UP, LEFT: OWN, DL: DOWN, UP: UR, OWN: RIGHT, DOWN: DR}, (UR, RIGHT, DR)),
+        (east, LEFT, UL, DL, {UR: UP, RIGHT: OWN, DR: DOWN, UP: UL, OWN: LEFT, DOWN: DL}, (UL, LEFT, DL)),
+    )
+
+    def start_mate(g):
+        for role, mate, over, under, _, _ in sides:
+            @pl.when(role)
+            def _(mate=mate):
+                r_wave[g, mate] = mate_wave[g]
+
+            start(mate_copy(g, 0, UP, under), role & there(UP))
+            start(mate_copy(g, 1, DOWN, over), role & there(DOWN))
 
     for g in range(GROUPS):
         if g > 0:
             for d in range(8):
-                arrived(wave_copy(g - 1, d, d), there(d))
-            for k in range(4):
-                for t in range(4):
-                    tile = TILE_SETS[k][t]
-                    new = wave[g - 1] if tile == OWN else r_wave[g - 1, tile]
-                    at = slice(k * NEAR + (g - 1) * PAD + t * 4, k * NEAR + (g - 1) * PAD + t * 4 + 4)
-                    call_f[at, :128] = new[:4, :]
-                    call_f[at, 128:] = new[4:, :]
-                at = slice(k * NEAR + (g - 1) * PAD, k * NEAR + g * PAD)
-                high, low = split(call_f[at, :])
-                c_high[at, :] = high
-                c_low[at, :] = low
-        product = mm(v_both, c_high[...])
-        coupled = product[:PAD] + product[PAD:] + mm(v_high, c_low[...])
-        chosen = (row_group == g) & (live_own > 0)
-        own = jnp.where(chosen, jnp.maximum(goal - coupled, 0.0), own)
+                arrived(wave_copy(g - 1, d, d), wave_ok(d))
+            for role, mate, over, under, _, _ in sides:
+                arrived(mate_copy(g - 1, 0, UP, over), role & there(UP))
+                arrived(mate_copy(g - 1, 1, DOWN, under), role & there(DOWN))
+            changes([r_wave[g - 1, d] for d in range(8)] + [wave[g - 1]], g - 1, call_f, c_high, c_low)
+        new = updated(g, goal, v_both, c_high, c_low, own, live_own)
         if g < GROUPS - 1:
-            wave[g, :4, :] = own[g * 4 : g * 4 + 4, :128]
-            wave[g, 4:, :] = own[g * 4 : g * 4 + 4, 128:]
+            pack(wave, g, new, own)
             for d in (UR, DR, UL, DL, RIGHT, LEFT, UP, DOWN):
-                start(wave_copy(g, d, 7 - d), there(d))
+                start(wave_copy(g, d, 7 - d), wave_ok(d))
+            if g < 2:
+                for down in (-1, 0, 1):
+                    start(far_copy(g, down, 2), beside_west & row_ok(down))
+                    start(far_copy(g, down, -2), beside_east & row_ok(down))
+        own = new
         if g == 0:
             for t in range(2):
                 arrived(piece_copy(t, DOWN), there(DOWN))
@@ -404,6 +488,50 @@
             below = (spot >> 6) < a_left
             merged[...] = jnp.where(below, r_piece[0].astype(I32), gather_tile(2).astype(I32)).astype(I16)
             start(remote(merged, r_merged, m_send, m_recv, LEFT), there(LEFT))
+
+            arrived(mate_share(3, 0, (0, 1)), west)
+            arrived(mate_share(1, 2, (1, 1)), west & row_ok(1))
+            arrived(mate_share(2, 1, (0, 2)), west)
+            arrived(mate_share(0, 3, (1, 2)), west & row_ok(1))
+            arrived(mate_share(3, 0, (0, -1)), east)
+            arrived(mate_share(1, 2, (1, -1)), east & row_ok(1))
+            arrived(mate_share(0, 3, (1, 0)), east & row_ok(1))
+
+            @pl.when(west)
+            def _():
+                mate_cm[...] = r_cm[RIGHT]
+
+            @pl.when(east)
+            def _():
+                mate_cm[...] = r_cm[LEFT]
+                r_mate[1] = share_out[2]
+
+            @pl.when(west | east)
+            def _():
+                live = mate_cm[:, FRAMES + 2 : FRAMES + 3]
+                mate_goal[...], mate_v[...] = joined([r_mate[k] for k in range(4)], live)
+                old = mate_cm[:, :FRAMES]
+                pack(mate_wave, 0, updated(0, mate_goal[...], None, None, None, old, live), old)
+
+            start_mate(0)
+        elif g < GROUPS - 1:
+            for down in (-1, 0, 1):
+                arrived(far_copy(g - 1, -down, 2), west & row_ok(down))
+                arrived(far_copy(g - 1, -down, -2), east & row_ok(down))
+            for role, mate, over, under, where_at, far_at in sides:
+                @pl.when(role)
+                def _(where_at=where_at, far_at=far_at):
+                    sources = {}
+                    for tile, at in where_at.items():
+                        sources[tile] = wave[g - 1] if at == OWN else r_wave[g - 1, at]
+                    for down, tile in enumerate(far_at):
+                        sources[tile] = r_far[g - 1, down]
+                    changes(sources, g - 1, mate_f, mate_high, mate_low)
+                    old = mate_cm[:, :FRAMES]
+                    live = mate_cm[:, FRAMES + 2 : FRAMES + 3]
+                    pack(mate_wave, g, updated(g, mate_goal[...], mate_v[...], mate_high, mate_low, old, live), old)
+
+            start_mate(g)
 
     back_own = jnp.dot(unpick16, own, precision=lax.Precision.HIGHEST, preferred_element_type=F32)
     new_traces = jnp.where(alive_sub[:SLOTS, 0:1], back_own[:SLOTS, :], old_traces)
@@ -446,12 +574,11 @@
             jax.ShapeDtypeStruct((SLOTS * PIX // 128, 128), F32),
             jax.ShapeDtypeStruct((SLOTS * FRAMES // 128, 128), F32),
         ),
-        in_specs=[pl.BlockSpec(memory_space=pl.ANY)] * 9,
+        in_specs=[pl.BlockSpec(memory_space=pltpu.SMEM)] + [pl.BlockSpec(memory_space=pltpu.HBM)] * 8,
         out_specs=(vmem, vmem),
         scratch_shapes=[
             pltpu.SMEM((2, SLOTS), I32),
             pltpu.SMEM((1, SLOTS), I32),
-            pltpu.SMEM((1, 1), I32),
             pltpu.SMEM((2,), I32),
             pltpu.VMEM((SLOTS * PIX // 128, 128), F32),
             pltpu.VMEM((SLOTS * FRAMES // 128, 128), F32),
@@ -479,15 +606,24 @@
             pltpu.VMEM((4 * NEAR, FRAMES), BF16),
             pltpu.VMEM((4 * NEAR, FRAMES), BF16),
             pltpu.VMEM((PAD, PIX), F32),
+            pltpu.VMEM((4, PAD, FRAMES + 128), F32),
+            pltpu.VMEM((PAD, FRAMES + 128), F32),
+            pltpu.VMEM((PAD, FRAMES), F32),
+            pltpu.VMEM((2 * PAD, 4 * NEAR), BF16),
+            pltpu.VMEM((3, 8, 128), F32),
+            pltpu.VMEM((2, 3, 8, 128), F32),
+            pltpu.VMEM((4 * NEAR, FRAMES), F32),
+            pltpu.VMEM((4 * NEAR, FRAMES), BF16),
+            pltpu.VMEM((4 * NEAR, FRAMES), BF16),
             pltpu.VMEM((2, PAD, PIX), I16),
             pltpu.VMEM((2, PAD, PIX), I16),
             pltpu.VMEM((PAD, PIX), I16),
             pltpu.VMEM((PAD, PIX), I16),
-            dma((9,)),
             dma((8,)),
             dma((8,)),
-            dma((3,)),
-            dma((3,)),
+            dma((8,)),
+            dma((3, HALVES)),
+            dma((3, HALVES)),
             dma((3,)),
             dma((3,)),
             dma((3, 8)),
@@ -496,18 +632,28 @@
             dma((2,)),
             dma,
             dma,
+            dma((4,)),
+            dma((4,)),
+            dma((3, 2)),
+            dma((2, 3)),
+            dma((2, 3)),
         ],
-        compiler_params=pltpu.CompilerParams(collective_id=0, has_side_effects=True),
+        compiler_params=pltpu.CompilerParams(collective_id=0, has_side_effects=True, vmem_limit_bytes=32 << 20),
     )(
-        anchors.reshape(SLOTS, 2).T,
-        groups.reshape(1, SLOTS),
         counts,
-        window,
-        footprints.reshape(SLOTS * PIX // 128, 128),
-        temporal.reshape(SLOTS * FRAMES // 128, 128),
-        back_spatial,
-        back_temporal,
-        movie.reshape(PIX, FRAMES),
+        *(
+            pltpu.with_memory_space_constraint(x, pltpu.HBM)
+            for x in (
+                anchors.reshape(SLOTS, 2).T,
+                groups.reshape(1, SLOTS),
+                window,
+                footprints.reshape(SLOTS * PIX // 128, 128),
+                temporal.reshape(SLOTS * FRAMES // 128, 128),
+                back_spatial,
+                back_temporal,
+                movie.reshape(PIX, FRAMES),
+            )
+        )
     )
     return shapes.reshape(1, 1, SLOTS, PIX), traces.reshape(1, 1, SLOTS, FRAMES)
 

time: 61 us -> 49.9 us (0.82)
  the two profiles are of different devices: /device:TPU:192 before, /device:TPU:129 now
where the time goes in v3:
time: 49.9 us; the launch traced here: 49.8 us
  Pallas kernels  47.2 us (95%)
  between operations  1.29 us (3%)
  local copies, waits for them, and re-layouts  1.28 us (3%)
    pallas_call x1, Pallas kernels, on_device(): pl.pallas_call(functools.partial(kernel, rows, cols), out_shape=(jax.Shap...  47.2 us
    unnamed x2, local copies, waits for them, and re-layouts  1.28 us

profile of v3, /device:TPU:129, one launch (start us, length us, event | category | flops | bytes accessed | tf_op | source)
XLA Modules:
  0.0 49.8 jit_solution(12618645307603194152)
XLA Ops:
  1.3 47.2 %shard_map.104 = (f32[384,128]{1,0:T(8,128)S(1)}, f32[24,128]{1,0:T(8,128)S(1)}) custom-call(s32[1,1]{1,0:T(1,128)S(6)} %copy.17.counts, s32[2,12]{1,0:T(2,128)} %bitcast.14, s32[1,12]{1,0:T(1,128)} %bitcast.15, s32[2]{0:T(128)} %window_in.1, f32[384,128]{1,0:T(8,128)} %bitcast.12, f32[24,128]{1,0:T(8,128)} %bitcast.13, bf16[2,64,64]{2,1,0:T(8,128)(2,1)} %back_in.1, ...), custom_call_target="tpu_custom_call" | custom-call | tf_op jit(solution)/shard_map/pallas_call | solution.py:571
  48.5 0.7 %copy.18 = f32[1,1,12,4096]{3,1,2,0:T(1,128)} copy(f32[1,1,12,4096]{3,1,2,0:T(1,128)S(1)} %bitcast.9) | data formatting | bytes 393216
  49.2 0.6 %copy.19 = f32[1,1,12,256]{3,1,2,0:T(1,128)} copy(f32[1,1,12,256]{3,1,2,0:T(1,128)S(1)} %bitcast.10) | data formatting | bytes 24576

commit v4 on v3

--- a/solution.py
+++ b/solution.py
@@ -21,6 +21,8 @@
 PAD = 16
 NEAR = 4 * PAD
 BIG = 1e30
+DENSE = 4 * SLOTS
+WIDE = PIX // 4
 TOP = 8.0
 
 DIRS = ((-1, -1), (-1, 0), (-1, 1), (0, -1), (0, 1), (1, -1), (1, 0), (1, 1))
@@ -32,7 +34,7 @@
     (LEFT, OWN, DL, DOWN),
     (OWN, RIGHT, DOWN, DR),
 )
-HALVES = 2
+PARTS = 4
 
 
 def nt(a, b):
@@ -69,12 +71,13 @@
     rows, cols,
     counts, anchors_in, groups_in, window_in, footprints_in, temporal_in, back_in, back_time_in, movie_in,
     out_shapes, out_traces,
-    anchors, groups, window, footprints, temporal, back_raw, back_time, movie, back_even, back, pad_f, hl, code, r_code, cm, r_cm, near_cm, target, canvas, x3,
-    shares, share_out, r_share, wave, r_wave, call_f, c_high, c_low, temp,
+    anchors, groups, window, footprints, temporal, back_raw, back_time, movie, back_even, back, pad_f, hl, code, code_right, r_code, cm, r_cm, near_cm, target, canvas, x3,
+    shares, share_out, r_share, wave, r_wave, call_f, c_high, c_low, temp, dense, labels, far_f, near_f,
     r_mate, mate_cm, mate_goal, mate_v, mate_wave, r_far, mate_f, mate_high, mate_low,
+    joint, r_joint, outer, r_outer, outer_wave, outer_f, outer_high, outer_low,
     piece_up, r_piece, merged, r_merged,
     load_sem, cm_send, cm_recv, r_send, r_recv, s_send, s_recv, t_send, t_recv, p_send, p_recv, m_send, m_recv,
-    mate_send, mate_recv, mw_send, far_send, far_recv,
+    mate_send, mate_recv, mw_send, far_send, far_recv, joint_sem, outer_sem, ow_send,
 ):
     r = lax.axis_index("row")
     c = lax.axis_index("col")
@@ -127,9 +130,14 @@
     call_f[...] = jnp.zeros_like(call_f)
     c_high[...] = jnp.zeros_like(c_high)
     c_low[...] = jnp.zeros_like(c_low)
+    far_f[...] = jnp.zeros_like(far_f)
+    near_f[...] = jnp.zeros_like(near_f)
     mate_f[...] = jnp.zeros_like(mate_f)
     mate_high[...] = jnp.zeros_like(mate_high)
     mate_low[...] = jnp.zeros_like(mate_low)
+    outer_f[...] = jnp.zeros_like(outer_f)
+    outer_high[...] = jnp.zeros_like(outer_high)
+    outer_low[...] = jnp.zeros_like(outer_low)
 
     expected = 0
     for d in range(8):
@@ -201,7 +209,25 @@
     for half in range(2):
         part = slice(half * 8, half * 8 + 8)
         pad_f[part, :] = turn(pad_f[part, :], shift_own[part], True)
-    code[...] = (pad_f[...] - 32768.0).astype(I32).astype(I16)
+
+    def packed(ref, row_of):
+        for q in range(4):
+            for g in range(GROUPS):
+                at = slice(q * SLOTS + g * 3, q * SLOTS + g * 3 + 3)
+                dense[at, :] = ref[row_of(g) : row_of(g) + 3, q * WIDE : (q + 1) * WIDE]
+        return dense[...].astype(I32).astype(I16)
+
+    def unpacked(codes, ref, row_of):
+        codes = codes.astype(I32).astype(F32)
+        for q in range(4):
+            for g in range(GROUPS):
+                at = slice(q * SLOTS + g * 3, q * SLOTS + g * 3 + 3)
+                ref[row_of(g) : row_of(g) + 3, q * WIDE : (q + 1) * WIDE] = codes[at, :]
+
+    pad_f[...] = pad_f[...] - 32768.0
+    code[...] = packed(pad_f, lambda g: g * 4)
+    temp[...] = half_turn(pad_f[...], False)
+    code_right[...] = packed(temp, lambda g: g * 4)
 
     loads[5].wait()
     loads[6].wait()
@@ -239,27 +265,29 @@
     def cm_copy(src, slot, d):
         return remote(src, r_cm.at[slot], cm_send.at[slot], cm_recv.at[slot], d)
 
-    for d in (RIGHT, LEFT, DOWN, UP):
-        start(cm_copy(cm, 7 - d, d), there(d))
-
     def code_copy(source, slot, part, d):
-        at = pl.ds(part * (PIX // HALVES), PIX // HALVES)
-        source = code.at[:, at] if source is None else r_code.at[source, :, at]
+        at = pl.ds(part * (WIDE // PARTS), WIDE // PARTS)
+        if source is None:
+            source = code_right.at[:, at] if slot == 2 else code.at[:, at]
+        else:
+            source = r_code.at[source, :, at]
         return remote(source, r_code.at[slot, :, at], r_send.at[slot, part], r_recv.at[slot, part], d)
 
-    for part in range(HALVES):
+    start(cm_copy(cm, LEFT, RIGHT), there(RIGHT))
+    for part in range(PARTS):
         start(code_copy(None, 2, part, RIGHT), there(RIGHT))
-    for part in range(HALVES):
+    start(cm_copy(cm, UP, DOWN), there(DOWN))
+    for part in range(PARTS):
         start(code_copy(None, 1, part, DOWN), there(DOWN))
+    start(cm_copy(cm, RIGHT, LEFT), east)
 
     arrived(cm_copy(cm, LEFT, LEFT), there(LEFT))
-    start(cm_copy(r_cm.at[LEFT], DL, UP), there(UP) & there(LEFT))
     start(cm_copy(r_cm.at[LEFT], UL, DOWN), there(DOWN) & there(LEFT))
-    arrived(cm_copy(cm, RIGHT, RIGHT), there(RIGHT))
-    start(cm_copy(r_cm.at[RIGHT], DR, UP), there(UP) & there(RIGHT))
-    start(cm_copy(r_cm.at[RIGHT], UR, DOWN), there(DOWN) & there(RIGHT))
-    for d in (UP, UL, DOWN, UR, DL, DR):
-        arrived(cm_copy(cm, d, d), there(d))
+    for part in range(PARTS):
+        arrived(code_copy(None, 2, part, LEFT), there(LEFT))
+        start(code_copy(2, 0, part, DOWN), there(DOWN) & there(LEFT))
+    arrived(cm_copy(cm, UP, UP), there(UP))
+    arrived(cm_copy(cm, UL, UL), there(UL))
 
     def cm_of(tile, rows_at, lanes_at):
         if tile == OWN:
@@ -313,19 +341,14 @@
         pull = pull - load0 * back[0:1, at] - load1 * back[1:2, at]
         target[:, at] = jnp.where(covered(slice(None), begin, width), pull * inverse, -BIG)
 
-    for part in range(HALVES):
-        arrived(code_copy(None, 2, part, LEFT), there(LEFT))
-        start(code_copy(2, 0, part, DOWN), there(DOWN) & there(LEFT))
-    for part in range(HALVES):
+    for part in range(PARTS):
         arrived(code_copy(None, 1, part, UP), there(UP))
-    for part in range(HALVES):
+    for part in range(PARTS):
         arrived(code_copy(None, 0, part, UL), there(UL))
-    for t in (0, 1, 2, 3):
-        coded = (r_code[t] if t < 3 else code[...]).astype(I32).astype(F32)
-        if t in (0, 2):
-            coded = half_turn(coded, False)
-        for g in range(GROUPS):
-            canvas[g * PAD + t * 4 : g * PAD + t * 4 + 4, :] = coded[g * 4 : g * 4 + 4, :]
+    for t in range(3):
+        unpacked(r_code[t], canvas, lambda g: g * PAD + t * 4)
+    for g in range(GROUPS):
+        canvas[g * PAD + 12 : g * PAD + 16, :] = pad_f[g * 4 : g * 4 + 4, :]
     for g in range(GROUPS):
         rows_at = slice(g * PAD, g * PAD + PAD)
         value = jnp.where(covered(rows_at, 0, PIX), (canvas[rows_at, :] + 32768.0) * (1.0 / 65535.0), 0.0)
@@ -355,7 +378,7 @@
     def share_copy(t, d):
         return remote(share_out.at[t], r_share.at[t], s_send.at[t], s_recv.at[t], d)
 
-    for t, d in ((0, UL), (2, LEFT), (1, UP)):
+    for t, d in ((2, LEFT), (0, UL), (1, UP)):
         start(share_copy(t, d), there(d))
 
     def mate_share(t, k, d):
@@ -363,11 +386,7 @@
 
     start(mate_share(3, 0, (0, 1)), west)
     start(mate_share(1, 2, (-1, 1)), west & row_ok(-1))
-    start(mate_share(3, 0, (0, -1)), east)
-    start(mate_share(1, 2, (-1, -1)), east & row_ok(-1))
     start(mate_share(0, 3, (-1, 0)), east & row_ok(-1))
-    start(mate_share(2, 1, (0, -2)), beside_east)
-    start(mate_share(0, 3, (-1, -2)), beside_east & row_ok(-1))
 
     for g in range(GROUPS):
         rows_at = slice(g * PAD, g * PAD + PAD)
@@ -379,19 +398,11 @@
             x3[NEAR + g * PAD : NEAR + g * PAD + PAD, :] = low
             x3[2 * NEAR + g * PAD : 2 * NEAR + g * PAD + PAD, :] = high
 
-    def gather_tile(t):
-        for g in range(GROUPS):
-            temp[g * 4 : g * 4 + 4, :] = canvas[g * PAD + t * 4 : g * PAD + t * 4 + 4, :]
-        return temp[...]
-
     for t in range(2):
-        piece_up[t] = gather_tile(t).astype(I32).astype(I16)
+        piece_up[t] = packed(canvas, lambda g: g * PAD + t * 4)
 
     def piece_copy(t, d):
         return remote(piece_up.at[t], r_piece.at[t], p_send.at[t], p_recv.at[t], d)
-
-    for t in range(2):
-        start(piece_copy(t, UP), there(UP))
 
     for t, d in ((2, RIGHT), (1, DOWN), (0, DR)):
         arrived(share_copy(t, d), there(d))
@@ -400,15 +411,21 @@
         total = parts[0] + parts[1] + parts[2] + parts[3]
         scale = 1.0 / jnp.where(live > 0, total[:, FRAMES + NEAR : FRAMES + NEAR + 1], 1.0)
         v = jnp.concatenate([part[:, FRAMES : FRAMES + NEAR] for part in parts], axis=1) * scale
-        return total[:, :FRAMES] * scale, jnp.concatenate(split(v), axis=0)
-
-    goal, v_both = joined([share_out[3], r_share[2], r_share[1], r_share[0]], live_own)
+        return total[:, :FRAMES] * scale, v
+
+    def stacked(v):
+        return jnp.concatenate(split(v), axis=0)
+
+    goal, v_own = joined([share_out[3], r_share[2], r_share[1], r_share[0]], live_own)
+    v_both = stacked(v_own)
     own = cm[:, :FRAMES]
     row_group = lax.broadcasted_iota(I32, (PAD, FRAMES), 0) >> 2
 
     def changes(sources, g, full, high_ref, low_ref):
         for k in range(4):
             for t in range(4):
+                if TILE_SETS[k][t] not in sources:
+                    continue
                 new = sources[TILE_SETS[k][t]]
                 at = slice(k * NEAR + g * PAD + t * 4, k * NEAR + g * PAD + t * 4 + 4)
                 full[at, :128] = new[:4, :]
@@ -418,11 +435,11 @@
             high_ref[at, :] = high
             low_ref[at, :] = low
 
-    def updated(g, aim, v_two, high_ref, low_ref, old, live):
-        left_over = aim
-        if g > 0:
-            product = mm(v_two, high_ref[...])
-            left_over = aim - (product[:PAD] + product[PAD:] + mm(v_two[:PAD], low_ref[...]))
+    def remaining(aim, v_two, high_ref, low_ref):
+        product = mm(v_two, high_ref[...])
+        return aim - (product[:PAD] + product[PAD:] + mm(v_two[:PAD], low_ref[...]))
+
+    def updated(g, left_over, old, live):
         chosen = (row_group == g) & (live > 0)
         return jnp.where(chosen, jnp.maximum(left_over, 0.0), old)
 
@@ -434,9 +451,17 @@
     def wave_copy(g, d, slot):
         return remote(wave.at[g], r_wave.at[g, slot], t_send.at[g, slot], t_recv.at[g, slot], d)
 
-    def wave_ok(d):
+    def sends(g, d):
         ok = there(d)
         if DIRS[d][1] > 0:
+            ok = ok & jnp.logical_not(west)
+        if DIRS[d][1] < 0 and g > 0:
+            ok = ok & jnp.logical_not(east)
+        return ok
+
+    def gets(g, d):
+        ok = there(d)
+        if DIRS[d][1] > 0 and g > 0:
             ok = ok & jnp.logical_not(west)
         if DIRS[d][1] < 0:
             ok = ok & jnp.logical_not(east)
@@ -448,13 +473,22 @@
     def far_copy(g, down, right):
         return remote(wave.at[g], r_far.at[g, 1 - down], far_send.at[g, 1 - down], far_recv.at[g, 1 - down], (down, right))
 
+    def outer_copy(at, d):
+        return remote(outer_wave, r_far.at[1, 2 - at], ow_send.at[at // 2], far_recv.at[1, 2 - at], d)
+
+    joint_copy = remote(joint, r_joint, joint_sem.at[0], joint_sem.at[1], LEFT)
+    outer_sum = remote(outer, r_outer, outer_sem.at[0], outer_sem.at[1], (0, 2))
+
     sides = (
-        (west, RIGHT, UR, DR, {UL: UP, LEFT: OWN, DL: DOWN, UP: UR, OWN: RIGHT, DOWN: DR}, (UR, RIGHT, DR)),
-        (east, LEFT, UL, DL, {UR: UP, RIGHT: OWN, DR: DOWN, UP: UL, OWN: LEFT, DOWN: DL}, (UL, LEFT, DL)),
+        (west, 1, RIGHT, UR, DR, {UL: UP, LEFT: OWN, DL: DOWN, UP: UR, OWN: RIGHT, DOWN: DR}, (UR, RIGHT, DR)),
+        (east, 0, LEFT, UL, DL, {UR: UP, RIGHT: OWN, DR: DOWN, UP: UL, OWN: LEFT, DOWN: DL}, (UL, LEFT, DL)),
     )
 
     def start_mate(g):
-        for role, mate, over, under, _, _ in sides:
+        for role, first, mate, over, under, _, _ in sides:
+            if g < first:
+                continue
+
             @pl.when(role)
             def _(mate=mate):
                 r_wave[g, mate] = mate_wave[g]
@@ -463,62 +497,99 @@
             start(mate_copy(g, 1, DOWN, over), role & there(DOWN))
 
     for g in range(GROUPS):
+        left_over = goal
         if g > 0:
-            for d in range(8):
-                arrived(wave_copy(g - 1, d, d), wave_ok(d))
-            for role, mate, over, under, _, _ in sides:
-                arrived(mate_copy(g - 1, 0, UP, over), role & there(UP))
-                arrived(mate_copy(g - 1, 1, DOWN, under), role & there(DOWN))
-            changes([r_wave[g - 1, d] for d in range(8)] + [wave[g - 1]], g - 1, call_f, c_high, c_low)
-        new = updated(g, goal, v_both, c_high, c_low, own, live_own)
+            for d in (UP, DOWN, LEFT, UL, DL):
+                arrived(wave_copy(g - 1, d, d), gets(g - 1, d))
+            if g == 1:
+                @pl.when(beside_west)
+                def _():
+                    sources = {d: r_wave[0, d] for d in (UP, DOWN, LEFT, UL, DL)}
+                    sources[OWN] = wave[0]
+                    changes(sources, 0, mate_f, mate_high, mate_low)
+                    aim = jnp.where(live_own > 0, remaining(goal, v_both, mate_high, mate_low), own)
+                    for at, value in enumerate((aim, own, v_own)):
+                        outer[at, :4, :] = value[4:8, :128]
+                        outer[at, 4:, :] = value[4:8, 128:]
+
+                start(outer_sum, beside_west)
+            for d in (RIGHT, UR, DR):
+                arrived(wave_copy(g - 1, d, d), gets(g - 1, d))
+            for role, first, mate, over, under, _, _ in sides:
+                if g - 1 >= first:
+                    arrived(mate_copy(g - 1, 0, UP, over), role & there(UP))
+                    arrived(mate_copy(g - 1, 1, DOWN, under), role & there(DOWN))
+            changes({**{d: r_wave[g - 1, d] for d in range(8)}, OWN: wave[g - 1]}, g - 1, call_f, c_high, c_low)
+            left_over = remaining(goal, v_both, c_high, c_low)
+        new = updated(g, left_over, own, live_own)
         if g < GROUPS - 1:
             pack(wave, g, new, own)
-            for d in (UR, DR, UL, DL, RIGHT, LEFT, UP, DOWN):
-                start(wave_copy(g, d, 7 - d), wave_ok(d))
+            for d in (UL, DL, LEFT, UR, DR, RIGHT, UP, DOWN):
+                start(wave_copy(g, d, 7 - d), sends(g, d))
             if g < 2:
                 for down in (-1, 0, 1):
-                    start(far_copy(g, down, 2), beside_west & row_ok(down))
+                    if g == 0:
+                        start(far_copy(g, down, 2), beside_west & row_ok(down))
                     start(far_copy(g, down, -2), beside_east & row_ok(down))
         own = new
         if g == 0:
+            @pl.when(east)
+            def _():
+                joint[:, :FRAMES] = goal
+                joint[:, FRAMES:] = v_own
+
+            start(joint_copy, east)
+
             for t in range(2):
-                arrived(piece_copy(t, DOWN), there(DOWN))
-            spot = lax.broadcasted_iota(I32, (PAD, PIX), 1)
-            a_left = r_cm[LEFT, :, FRAMES : FRAMES + 1].astype(I32)
-            below = (spot >> 6) < a_left
-            merged[...] = jnp.where(below, r_piece[0].astype(I32), gather_tile(2).astype(I32)).astype(I16)
-            start(remote(merged, r_merged, m_send, m_recv, LEFT), there(LEFT))
-
-            arrived(mate_share(3, 0, (0, 1)), west)
-            arrived(mate_share(1, 2, (1, 1)), west & row_ok(1))
-            arrived(mate_share(2, 1, (0, 2)), west)
-            arrived(mate_share(0, 3, (1, 2)), west & row_ok(1))
+                start(piece_copy(t, UP), there(UP))
+
             arrived(mate_share(3, 0, (0, -1)), east)
             arrived(mate_share(1, 2, (1, -1)), east & row_ok(1))
             arrived(mate_share(0, 3, (1, 0)), east & row_ok(1))
-
-            @pl.when(west)
-            def _():
-                mate_cm[...] = r_cm[RIGHT]
 
             @pl.when(east)
             def _():
                 mate_cm[...] = r_cm[LEFT]
                 r_mate[1] = share_out[2]
-
-            @pl.when(west | east)
-            def _():
                 live = mate_cm[:, FRAMES + 2 : FRAMES + 3]
-                mate_goal[...], mate_v[...] = joined([r_mate[k] for k in range(4)], live)
+                mate_goal[...], v_mate = joined([r_mate[k] for k in range(4)], live)
+                mate_v[...] = stacked(v_mate)
                 old = mate_cm[:, :FRAMES]
-                pack(mate_wave, 0, updated(0, mate_goal[...], None, None, None, old, live), old)
+                pack(mate_wave, 0, updated(0, mate_goal[...], old, live), old)
 
             start_mate(0)
+
+            for q in range(4):
+                for k in range(GROUPS):
+                    at = slice(q * SLOTS + k * 3, q * SLOTS + k * 3 + 3)
+                    labels[at, :] = r_cm[LEFT, k * 4 : k * 4 + 3, FRAMES:]
+            a_left = labels[:, 0:1].astype(I32)
+            row = lax.broadcasted_iota(I32, (DENSE, WIDE), 0)
+            quarter = (row >= SLOTS).astype(I32) + (row >= 2 * SLOTS).astype(I32) + (row >= 3 * SLOTS).astype(I32)
+            below = quarter * 16 + (lax.broadcasted_iota(I32, (DENSE, WIDE), 1) >> 6) < a_left
+            left_codes = packed(canvas, lambda k: k * PAD + 8).astype(I32)
+            for t in range(2):
+                arrived(piece_copy(t, DOWN), there(DOWN))
+            merged[...] = jnp.where(below, r_piece[0].astype(I32), left_codes).astype(I16)
+            start(remote(merged, r_merged, m_send, m_recv, LEFT), there(LEFT))
         elif g < GROUPS - 1:
+            if g == 1:
+                arrived(cm_copy(cm, RIGHT, RIGHT), west)
+                arrived(joint_copy, west)
+
+                @pl.when(west)
+                def _():
+                    mate_cm[...] = r_cm[RIGHT]
+                    mate_goal[...] = r_joint[:, :FRAMES]
+                    mate_v[...] = stacked(r_joint[:, FRAMES:])
+
             for down in (-1, 0, 1):
-                arrived(far_copy(g - 1, -down, 2), west & row_ok(down))
-                arrived(far_copy(g - 1, -down, -2), east & row_ok(down))
-            for role, mate, over, under, where_at, far_at in sides:
+                arrived(far_copy(g - 1, -down, -2), west & row_ok(down))
+                if g == 1:
+                    arrived(far_copy(g - 1, -down, 2), east & row_ok(down))
+                elif down:
+                    arrived(outer_copy(1 - down, (down, 0)), east & row_ok(down))
+            for role, first, mate, over, under, where_at, far_at in sides:
                 @pl.when(role)
                 def _(where_at=where_at, far_at=far_at):
                     sources = {}
@@ -529,9 +600,31 @@
                     changes(sources, g - 1, mate_f, mate_high, mate_low)
                     old = mate_cm[:, :FRAMES]
                     live = mate_cm[:, FRAMES + 2 : FRAMES + 3]
-                    pack(mate_wave, g, updated(g, mate_goal[...], mate_v[...], mate_high, mate_low, old, live), old)
+                    rest = remaining(mate_goal[...], mate_v[...], mate_high, mate_low)
+                    pack(mate_wave, g, updated(g, rest, old, live), old)
 
             start_mate(g)
+            if g == 1:
+                arrived(outer_sum, east)
+
+                @pl.when(east)
+                def _():
+                    changes({UR: r_wave[0, UL], RIGHT: r_wave[0, LEFT], DR: r_wave[0, DL]}, 0, outer_f, outer_high, outer_low)
+                    zero = jnp.zeros((4, FRAMES), F32)
+                    aim, old, v = (
+                        jnp.concatenate(
+                            [zero, jnp.concatenate([r_outer[at, :4, :], r_outer[at, 4:, :]], axis=1), zero, zero], axis=0
+                        )
+                        for at in range(3)
+                    )
+                    value = jnp.maximum(remaining(aim, stacked(v), outer_high, outer_low), 0.0)
+                    pack2 = value - old
+                    outer_wave[:4, :] = pack2[4:8, :128]
+                    outer_wave[4:, :] = pack2[4:8, 128:]
+                    r_far[1, 1] = outer_wave[...]
+
+                start(outer_copy(0, UP), east & there(UP))
+                start(outer_copy(2, DOWN), east & there(DOWN))
 
     back_own = jnp.dot(unpick16, own, precision=lax.Precision.HIGHEST, preferred_element_type=F32)
     new_traces = jnp.where(alive_sub[:SLOTS, 0:1], back_own[:SLOTS, :], old_traces)
@@ -539,13 +632,17 @@
         out_traces[pl.ds(half, SLOTS, stride=2), :] = new_traces[:, half * 128 : half * 128 + 128]
 
     arrived(remote(merged, r_merged, m_send, m_recv, RIGHT), there(RIGHT))
+    spot = lax.broadcasted_iota(I32, (PAD, PIX), 1)
     y = spot >> 6
     x = spot & 63
     a_int = a_own.astype(I32)
     b_int = b_own.astype(I32)
-    far = half_turn(r_merged[...].astype(I32).astype(F32), True)
-    near = jnp.where(y < a_int, r_piece[1].astype(I32).astype(F32), gather_tile(3))
-    pad_f[...] = jnp.where(x < b_int, far, near) + 32768.0
+    unpacked(r_merged[...], far_f, lambda g: g * 4)
+    unpacked(r_piece[1], near_f, lambda g: g * 4)
+    for g in range(GROUPS):
+        temp[g * 4 : g * 4 + 4, :] = canvas[g * PAD + 12 : g * PAD + 16, :]
+    near = jnp.where(y < a_int, near_f[...], temp[...])
+    pad_f[...] = jnp.where(x < b_int, half_turn(far_f[...], True), near) + 32768.0
     for half in range(2):
         part = slice(half * 8, half * 8 + 8)
         pad_f[part, :] = turn(pad_f[part, :], shift_own[part], False)
@@ -589,8 +686,9 @@
             pltpu.VMEM((8, PIX), F32),
             pltpu.VMEM((PAD, PIX), F32),
             pltpu.VMEM((2 * PAD, PIX), BF16),
-            pltpu.VMEM((PAD, PIX), I16),
-            pltpu.VMEM((3, PAD, PIX), I16),
+            pltpu.VMEM((DENSE, WIDE), I16),
+            pltpu.VMEM((DENSE, WIDE), I16),
+            pltpu.VMEM((3, DENSE, WIDE), I16),
             pltpu.VMEM((PAD, FRAMES + 128), F32),
             pltpu.VMEM((8, PAD, FRAMES + 128), F32),
             pltpu.VMEM((NEAR, FRAMES + 128), F32),
@@ -606,6 +704,10 @@
             pltpu.VMEM((4 * NEAR, FRAMES), BF16),
             pltpu.VMEM((4 * NEAR, FRAMES), BF16),
             pltpu.VMEM((PAD, PIX), F32),
+            pltpu.VMEM((DENSE, WIDE), F32),
+            pltpu.VMEM((DENSE, 128), F32),
+            pltpu.VMEM((PAD, PIX), F32),
+            pltpu.VMEM((PAD, PIX), F32),
             pltpu.VMEM((4, PAD, FRAMES + 128), F32),
             pltpu.VMEM((PAD, FRAMES + 128), F32),
             pltpu.VMEM((PAD, FRAMES), F32),
@@ -615,15 +717,23 @@
             pltpu.VMEM((4 * NEAR, FRAMES), F32),
             pltpu.VMEM((4 * NEAR, FRAMES), BF16),
             pltpu.VMEM((4 * NEAR, FRAMES), BF16),
-            pltpu.VMEM((2, PAD, PIX), I16),
-            pltpu.VMEM((2, PAD, PIX), I16),
-            pltpu.VMEM((PAD, PIX), I16),
-            pltpu.VMEM((PAD, PIX), I16),
+            pltpu.VMEM((PAD, 2 * FRAMES), F32),
+            pltpu.VMEM((PAD, 2 * FRAMES), F32),
+            pltpu.VMEM((3, 8, 128), F32),
+            pltpu.VMEM((3, 8, 128), F32),
+            pltpu.VMEM((8, 128), F32),
+            pltpu.VMEM((4 * NEAR, FRAMES), F32),
+            pltpu.VMEM((4 * NEAR, FRAMES), BF16),
+            pltpu.VMEM((4 * NEAR, FRAMES), BF16),
+            pltpu.VMEM((2, DENSE, WIDE), I16),
+            pltpu.VMEM((2, DENSE, WIDE), I16),
+            pltpu.VMEM((DENSE, WIDE), I16),
+            pltpu.VMEM((DENSE, WIDE), I16),
             dma((8,)),
             dma((8,)),
             dma((8,)),
-            dma((3, HALVES)),
-            dma((3, HALVES)),
+            dma((3, PARTS)),
+            dma((3, PARTS)),
             dma((3,)),
             dma((3,)),
             dma((3, 8)),
@@ -637,6 +747,9 @@
             dma((3, 2)),
             dma((2, 3)),
             dma((2, 3)),
+            dma((2,)),
+            dma((2,)),
+            dma((2,)),
         ],
         compiler_params=pltpu.CompilerParams(collective_id=0, has_side_effects=True, vmem_limit_bytes=32 << 20),
     )(

time: 49.9 us -> 47.9 us (0.960)
  the two profiles are of different devices: /device:TPU:129 before, /device:TPU:15 now
where the time goes in v4:
time: 47.9 us; the launch traced here: 47.8 us
  Pallas kernels  45.2 us (94%)
  between operations  1.29 us (3%)
  local copies, waits for them, and re-layouts  1.28 us (3%)
    pallas_call x1, Pallas kernels, on_device(): pl.pallas_call(functools.partial(kernel, rows, cols), out_shape=(jax.Shap...  45.2 us
    unnamed x2, local copies, waits for them, and re-layouts  1.28 us

profile of v4, /device:TPU:15, one launch (start us, length us, event | category | flops | bytes accessed | tf_op | source)
XLA Modules:
  0.0 47.8 jit_solution(1073642255889412350)
XLA Ops:
  1.3 45.2 %shard_map.104 = (f32[384,128]{1,0:T(8,128)S(1)}, f32[24,128]{1,0:T(8,128)S(1)}) custom-call(s32[1,1]{1,0:T(1,128)S(6)} %copy.17.counts, s32[2,12]{1,0:T(2,128)} %bitcast.14, s32[1,12]{1,0:T(1,128)} %bitcast.15, s32[2]{0:T(128)} %window_in.1, f32[384,128]{1,0:T(8,128)} %bitcast.12, f32[24,128]{1,0:T(8,128)} %bitcast.13, bf16[2,64,64]{2,1,0:T(8,128)(2,1)} %back_in.1, ...), custom_call_target="tpu_custom_call" | custom-call | tf_op jit(solution)/shard_map/pallas_call | solution.py:668
  46.5 0.7 %copy.18 = f32[1,1,12,4096]{3,1,2,0:T(1,128)} copy(f32[1,1,12,4096]{3,1,2,0:T(1,128)S(1)} %bitcast.9) | data formatting | bytes 393216
  47.2 0.6 %copy.19 = f32[1,1,12,256]{3,1,2,0:T(1,128)} copy(f32[1,1,12,256]{3,1,2,0:T(1,128)S(1)} %bitcast.10) | data formatting | bytes 24576

commit v5 on v4

--- a/solution.py
+++ b/solution.py
@@ -404,6 +404,9 @@
     def piece_copy(t, d):
         return remote(piece_up.at[t], r_piece.at[t], p_send.at[t], p_recv.at[t], d)
 
+    for t in range(2):
+        start(piece_copy(t, UP), there(UP) & (c < cols // 2))
+
     for t, d in ((2, RIGHT), (1, DOWN), (0, DR)):
         arrived(share_copy(t, d), there(d))
 
@@ -498,6 +501,32 @@
 
     for g in range(GROUPS):
         left_over = goal
+        if g == GROUPS - 1:
+            arrived(remote(merged, r_merged, m_send, m_recv, RIGHT), there(RIGHT))
+            spot = lax.broadcasted_iota(I32, (PAD, PIX), 1)
+            y = spot >> 6
+            x = spot & 63
+            a_int = a_own.astype(I32)
+            b_int = b_own.astype(I32)
+            unpacked(r_merged[...], far_f, lambda k: k * 4)
+            unpacked(r_piece[1], near_f, lambda k: k * 4)
+            for k in range(GROUPS):
+                temp[k * 4 : k * 4 + 4, :] = canvas[k * PAD + 12 : k * PAD + 16, :]
+            near = jnp.where(y < a_int, near_f[...], temp[...])
+            pad_f[...] = jnp.where(x < b_int, half_turn(far_f[...], True), near) + 32768.0
+            for half in range(2):
+                part = slice(half * 8, half * 8 + 8)
+                pad_f[part, :] = turn(pad_f[part, :], shift_own[part], False)
+            whole = pad_f[...]
+            upper = jnp.floor(whole * (1.0 / 256.0))
+            hl[:PAD, :] = upper.astype(BF16)
+            hl[PAD:, :] = (whole - upper * 256.0).astype(BF16)
+            unpick_hl = jnp.concatenate([unpick16 * 256.0, unpick16], axis=1).astype(BF16)
+            root = mm(unpick_hl, hl[...])[:SLOTS, :] * (1.0 / 65535.0)
+            pad_f[:SLOTS, :] = root * root * TOP
+            for q in range(PIX // 128):
+                out_shapes[pl.ds(q, SLOTS, stride=32), :] = pad_f[:SLOTS, q * 128 : q * 128 + 128]
+
         if g > 0:
             for d in (UP, DOWN, LEFT, UL, DL):
                 arrived(wave_copy(g - 1, d, d), gets(g - 1, d))
@@ -541,7 +570,7 @@
             start(joint_copy, east)
 
             for t in range(2):
-                start(piece_copy(t, UP), there(UP))
+                start(piece_copy(t, UP), there(UP) & (c >= cols // 2))
 
             arrived(mate_share(3, 0, (0, -1)), east)
             arrived(mate_share(1, 2, (1, -1)), east & row_ok(1))
@@ -630,31 +659,6 @@
     new_traces = jnp.where(alive_sub[:SLOTS, 0:1], back_own[:SLOTS, :], old_traces)
     for half in range(2):
         out_traces[pl.ds(half, SLOTS, stride=2), :] = new_traces[:, half * 128 : half * 128 + 128]
-
-    arrived(remote(merged, r_merged, m_send, m_recv, RIGHT), there(RIGHT))
-    spot = lax.broadcasted_iota(I32, (PAD, PIX), 1)
-    y = spot >> 6
-    x = spot & 63
-    a_int = a_own.astype(I32)
-    b_int = b_own.astype(I32)
-    unpacked(r_merged[...], far_f, lambda g: g * 4)
-    unpacked(r_piece[1], near_f, lambda g: g * 4)
-    for g in range(GROUPS):
-        temp[g * 4 : g * 4 + 4, :] = canvas[g * PAD + 12 : g * PAD + 16, :]
-    near = jnp.where(y < a_int, near_f[...], temp[...])
-    pad_f[...] = jnp.where(x < b_int, half_turn(far_f[...], True), near) + 32768.0
-    for half in range(2):
-        part = slice(half * 8, half * 8 + 8)
-        pad_f[part, :] = turn(pad_f[part, :], shift_own[part], False)
-    whole = pad_f[...]
-    upper = jnp.floor(whole * (1.0 / 256.0))
-    hl[:PAD, :] = upper.astype(BF16)
-    hl[PAD:, :] = (whole - upper * 256.0).astype(BF16)
-    unpick_hl = jnp.concatenate([unpick16 * 256.0, unpick16], axis=1).astype(BF16)
-    root = mm(unpick_hl, hl[...])[:SLOTS, :] * (1.0 / 65535.0)
-    pad_f[:SLOTS, :] = root * root * TOP
-    for q in range(PIX // 128):
-        out_shapes[pl.ds(q, SLOTS, stride=32), :] = pad_f[:SLOTS, q * 128 : q * 128 + 128]
 
     for copy, ok in pending:
         @pl.when(ok)

time: 47.9 us -> 45.3 us (0.946)
  the two profiles are of different devices: /device:TPU:15 before, /device:TPU:7 now
where the time goes in v5:
time: 45.3 us; the launch traced here: 45.2 us
  Pallas kernels  42.6 us (94%)
  between operations  1.29 us (3%)
  local copies, waits for them, and re-layouts  1.28 us (3%)
    pallas_call x1, Pallas kernels, on_device(): pl.pallas_call(functools.partial(kernel, rows, cols), out_shape=(jax.Shap...  42.6 us
    unnamed x2, local copies, waits for them, and re-layouts  1.28 us

profile of v5, /device:TPU:7, one launch (start us, length us, event | category | flops | bytes accessed | tf_op | source)
XLA Modules:
  0.0 45.2 jit_solution(9877636950363379727)
XLA Ops:
  1.3 42.6 %shard_map.104 = (f32[384,128]{1,0:T(8,128)S(1)}, f32[24,128]{1,0:T(8,128)S(1)}) custom-call(s32[1,1]{1,0:T(1,128)S(6)} %copy.17.counts, s32[2,12]{1,0:T(2,128)} %bitcast.14, s32[1,12]{1,0:T(1,128)} %bitcast.15, s32[2]{0:T(128)} %window_in.1, f32[384,128]{1,0:T(8,128)} %bitcast.12, f32[24,128]{1,0:T(8,128)} %bitcast.13, bf16[2,64,64]{2,1,0:T(8,128)(2,1)} %back_in.1, ...), custom_call_target="tpu_custom_call" | custom-call | tf_op jit(solution)/shard_map/pallas_call | solution.py:672
  43.9 0.7 %copy.18 = f32[1,1,12,4096]{3,1,2,0:T(1,128)} copy(f32[1,1,12,4096]{3,1,2,0:T(1,128)S(1)} %bitcast.9) | data formatting | bytes 393216
  44.6 0.6 %copy.19 = f32[1,1,12,256]{3,1,2,0:T(1,128)} copy(f32[1,1,12,256]{3,1,2,0:T(1,128)S(1)} %bitcast.10) | data formatting | bytes 24576

commit v6 on v5

--- a/solution.py
+++ b/solution.py
@@ -122,23 +122,6 @@
     for load in loads:
         load.start()
 
-    r_cm[...] = jnp.zeros_like(r_cm)
-    r_share[...] = jnp.zeros_like(r_share)
-    r_wave[...] = jnp.zeros_like(r_wave)
-    r_mate[...] = jnp.zeros_like(r_mate)
-    r_far[...] = jnp.zeros_like(r_far)
-    call_f[...] = jnp.zeros_like(call_f)
-    c_high[...] = jnp.zeros_like(c_high)
-    c_low[...] = jnp.zeros_like(c_low)
-    far_f[...] = jnp.zeros_like(far_f)
-    near_f[...] = jnp.zeros_like(near_f)
-    mate_f[...] = jnp.zeros_like(mate_f)
-    mate_high[...] = jnp.zeros_like(mate_high)
-    mate_low[...] = jnp.zeros_like(mate_low)
-    outer_f[...] = jnp.zeros_like(outer_f)
-    outer_high[...] = jnp.zeros_like(outer_high)
-    outer_low[...] = jnp.zeros_like(outer_low)
-
     expected = 0
     for d in range(8):
         ok = there(d)
@@ -149,14 +132,38 @@
 
         expected = expected + ok.astype(I32)
     for down in (-1, 0, 1):
-        for right, role in ((2, beside_west | west), (-2, beside_east | east)):
-            ok = role & row_ok(down)
-
-            @pl.when(ok)
+        for right, receiver, sender in ((2, west, beside_east), (-2, east, beside_west)):
+            @pl.when(receiver & row_ok(down))
             def _(down=down, right=right):
                 pl.semaphore_signal(barrier, inc=1, device_id=(r + down, c + right), device_id_type=MESH)
 
-            expected = expected + ok.astype(I32)
+            expected = expected + (sender & row_ok(down)).astype(I32)
+
+    for d in range(8):
+        @pl.when(jnp.logical_not(there(d)))
+        def _(d=d):
+            r_cm[d] = jnp.zeros((PAD, FRAMES + 128), F32)
+            for g in range(3):
+                r_wave[g, d] = jnp.zeros((8, 128), F32)
+
+    for t, d in ((0, DR), (1, DOWN), (2, RIGHT)):
+        @pl.when(jnp.logical_not(there(d)))
+        def _(t=t):
+            r_share[t] = jnp.zeros((PAD, FRAMES + 128), F32)
+
+    @pl.when(jnp.logical_not(row_ok(1)))
+    def _():
+        r_mate[2] = jnp.zeros((PAD, FRAMES + 128), F32)
+        r_mate[3] = jnp.zeros((PAD, FRAMES + 128), F32)
+
+    for down in (-1, 1):
+        @pl.when(jnp.logical_not(row_ok(down)))
+        def _(down=down):
+            for g in range(2):
+                r_far[g, 1 + down] = jnp.zeros((8, 128), F32)
+
+    for ref in (call_f, c_high, c_low, far_f, near_f, mate_f, mate_high, mate_low, outer_f, outer_high, outer_low):
+        ref[...] = jnp.zeros_like(ref)
 
     for load in loads[:4]:
         load.wait()
@@ -238,7 +245,8 @@
     back_even[:SIDE, :] = jnp.concatenate([even, odd], axis=1)
     for q in range(PIX // 128):
         back[:2, q * 128 : q * 128 + 128] = back_even[pl.ds(q, 2, stride=32), :]
-    back[2:, :] = jnp.zeros((6, PIX), F32)
+    back[2:, :] = jnp.zeros((14, PIX), F32)
+    x3[3 * NEAR :, :] = back[...].astype(BF16)
 
     pl.semaphore_wait(barrier, expected)
 
@@ -357,11 +365,10 @@
         x3[NEAR + g * PAD : NEAR + g * PAD + PAD, :] = low
         x3[2 * NEAR + g * PAD : 2 * NEAR + g * PAD + PAD, :] = high
 
-    both = x3[: 2 * NEAR, :]
-    gram = nt(both, both)
-    overlap = gram[:NEAR, :NEAR] + gram[:NEAR, NEAR:] + gram[NEAR:, :NEAR] + gram[NEAR:, NEAR:]
-    loading = nt(both, back[...].astype(BF16))
-    loading = loading[:NEAR] + loading[NEAR:]
+    gram = nt(x3[: 2 * NEAR, :], x3[NEAR:, :])
+    gram = gram[:NEAR] + gram[NEAR:]
+    overlap = gram[:, :NEAR] + gram[:, NEAR : 2 * NEAR]
+    loading = gram[:, 2 * NEAR : 2 * NEAR + 2]
     drive = mm(x3[:NEAR, :], movie[...])
     drive = drive - loading[:, 0:1] * back_time[0:1, :] - loading[:, 1:2] * back_time[1:2, :]
     self_overlap = jnp.sum(jnp.where(eye, overlap, 0.0), axis=1, keepdims=True)
@@ -390,7 +397,7 @@
 
     for g in range(GROUPS):
         rows_at = slice(g * PAD, g * PAD + PAD)
-        value = jnp.maximum(target[rows_at, :] - mm(q3[rows_at, :], x3[...]), 0.0)
+        value = jnp.maximum(target[rows_at, :] - mm(q3[rows_at, :], x3[: 3 * NEAR, :]), 0.0)
         canvas[rows_at, :] = jnp.floor(jnp.sqrt(value * (1.0 / TOP)) * 65535.0 + 0.5) - 32768.0
         if g < GROUPS - 1:
             high, low = split(value)
@@ -687,7 +694,7 @@
             pltpu.VMEM((2, FRAMES), F32),
             pltpu.VMEM((PIX, FRAMES), BF16),
             pltpu.VMEM((2 * SIDE, 2 * SIDE), F32),
-            pltpu.VMEM((8, PIX), F32),
+            pltpu.VMEM((16, PIX), F32),
             pltpu.VMEM((PAD, PIX), F32),
             pltpu.VMEM((2 * PAD, PIX), BF16),
             pltpu.VMEM((DENSE, WIDE), I16),
@@ -698,7 +705,7 @@
             pltpu.VMEM((NEAR, FRAMES + 128), F32),
             pltpu.VMEM((NEAR, PIX), F32),
             pltpu.VMEM((NEAR, PIX), F32),
-            pltpu.VMEM((3 * NEAR, PIX), BF16),
+            pltpu.VMEM((3 * NEAR + 16, PIX), BF16),
             pltpu.VMEM((NEAR, FRAMES + 128), F32),
             pltpu.VMEM((4, PAD, FRAMES + 128), F32),
             pltpu.VMEM((3, PAD, FRAMES + 128), F32),

time: 45.3 us -> 43.5 us (0.960)
  Pallas kernels: 42.6 us -> 40.8 us
    pallas_call x1, Pallas kernels: 42.6 us -> 40.8 us  [on_device(): pl.pallas_call(functools.partial(kernel, rows, cols), out_shape=(jax.Shap...]
where the time goes in v6:
time: 43.5 us; the launch traced here: 43.4 us
  Pallas kernels  40.8 us (94%)
  between operations  1.29 us (3%)
  local copies, waits for them, and re-layouts  1.28 us (3%)
    pallas_call x1, Pallas kernels, on_device(): pl.pallas_call(functools.partial(kernel, rows, cols), out_shape=(jax.Shap...  40.8 us
    unnamed x2, local copies, waits for them, and re-layouts  1.28 us

profile of v6, /device:TPU:7, one launch (start us, length us, event | category | flops | bytes accessed | tf_op | source)
XLA Modules:
  0.0 43.4 jit_solution(1108726621533850507)
XLA Ops:
  1.3 40.8 %shard_map.104 = (f32[384,128]{1,0:T(8,128)S(1)}, f32[24,128]{1,0:T(8,128)S(1)}) custom-call(s32[1,1]{1,0:T(1,128)S(6)} %copy.17.counts, s32[2,12]{1,0:T(2,128)} %bitcast.14, s32[1,12]{1,0:T(1,128)} %bitcast.15, s32[2]{0:T(128)} %window_in.1, f32[384,128]{1,0:T(8,128)} %bitcast.12, f32[24,128]{1,0:T(8,128)} %bitcast.13, bf16[2,64,64]{2,1,0:T(8,128)(2,1)} %back_in.1, ...), custom_call_target="tpu_custom_call" | custom-call | tf_op jit(solution)/shard_map/pallas_call | solution.py:679
  42.1 0.7 %copy.18 = f32[1,1,12,4096]{3,1,2,0:T(1,128)} copy(f32[1,1,12,4096]{3,1,2,0:T(1,128)S(1)} %bitcast.9) | data formatting | bytes 393216
  42.8 0.6 %copy.19 = f32[1,1,12,256]{3,1,2,0:T(1,128)} copy(f32[1,1,12,256]{3,1,2,0:T(1,128)S(1)} %bitcast.10) | data formatting | bytes 24576

commit v7 on v6

--- a/solution.py
+++ b/solution.py
@@ -125,12 +125,14 @@
     expected = 0
     for d in range(8):
         ok = there(d)
-
-        @pl.when(ok)
+        hears = ok & jnp.logical_not(west) if d in (UR, DR) else ok
+        tells = ok & jnp.logical_not(east) if d in (UL, DL) else ok
+
+        @pl.when(tells)
         def _(d=d):
             pl.semaphore_signal(barrier, inc=1, device_id=place(d), device_id_type=MESH)
 
-        expected = expected + ok.astype(I32)
+        expected = expected + hears.astype(I32)
     for down in (-1, 0, 1):
         for right, receiver, sender in ((2, west, beside_east), (-2, east, beside_west)):
             @pl.when(receiver & row_ok(down))
@@ -284,9 +286,12 @@
     start(cm_copy(cm, LEFT, RIGHT), there(RIGHT))
     for part in range(PARTS):
         start(code_copy(None, 2, part, RIGHT), there(RIGHT))
-    start(cm_copy(cm, UP, DOWN), there(DOWN))
-    for part in range(PARTS):
-        start(code_copy(None, 1, part, DOWN), there(DOWN))
+    def own_down(role):
+        start(cm_copy(cm, UP, DOWN), there(DOWN) & role)
+        for part in range(PARTS):
+            start(code_copy(None, 1, part, DOWN), there(DOWN) & role)
+
+    own_down(jnp.logical_not(west))
     start(cm_copy(cm, RIGHT, LEFT), east)
 
     arrived(cm_copy(cm, LEFT, LEFT), there(LEFT))
@@ -294,6 +299,7 @@
     for part in range(PARTS):
         arrived(code_copy(None, 2, part, LEFT), there(LEFT))
         start(code_copy(2, 0, part, DOWN), there(DOWN) & there(LEFT))
+    own_down(west)
     arrived(cm_copy(cm, UP, UP), there(UP))
     arrived(cm_copy(cm, UL, UL), there(UL))
 
@@ -392,7 +398,6 @@
         return remote(share_out.at[t], r_mate.at[k], mate_send.at[t], mate_recv.at[k], d)
 
     start(mate_share(3, 0, (0, 1)), west)
-    start(mate_share(1, 2, (-1, 1)), west & row_ok(-1))
     start(mate_share(0, 3, (-1, 0)), east & row_ok(-1))
 
     for g in range(GROUPS):
@@ -414,7 +419,9 @@
     for t in range(2):
         start(piece_copy(t, UP), there(UP) & (c < cols // 2))
 
-    for t, d in ((2, RIGHT), (1, DOWN), (0, DR)):
+    arrived(share_copy(1, DOWN), there(DOWN))
+    start(remote(r_share.at[1], r_mate.at[2], mate_send.at[1], mate_recv.at[2], RIGHT), west & row_ok(1))
+    for t, d in ((2, RIGHT), (0, DR)):
         arrived(share_copy(t, d), there(d))
 
     def joined(parts, live):
@@ -580,7 +587,7 @@
                 start(piece_copy(t, UP), there(UP) & (c >= cols // 2))
 
             arrived(mate_share(3, 0, (0, -1)), east)
-            arrived(mate_share(1, 2, (1, -1)), east & row_ok(1))
+            arrived(mate_share(1, 2, (0, -1)), east & row_ok(1))
             arrived(mate_share(0, 3, (1, 0)), east & row_ok(1))
 
             @pl.when(east)

time: 43.5 us -> 42.3 us (0.972)
  Pallas kernels: 40.8 us -> 39.7 us
    pallas_call x1, Pallas kernels: 40.8 us -> 39.7 us  [on_device(): pl.pallas_call(functools.partial(kernel, rows, cols), out_shape=(jax.Shap...]
where the time goes in v7:
time: 42.3 us; the launch traced here: 42.2 us
  Pallas kernels  39.7 us (94%)
  between operations  1.29 us (3%)
  local copies, waits for them, and re-layouts  1.28 us (3%)
    pallas_call x1, Pallas kernels, on_device(): pl.pallas_call(functools.partial(kernel, rows, cols), out_shape=(jax.Shap...  39.7 us
    unnamed x2, local copies, waits for them, and re-layouts  1.28 us

profile of v7, /device:TPU:7, one launch (start us, length us, event | category | flops | bytes accessed | tf_op | source)
XLA Modules:
  0.0 42.2 jit_solution(3938288686049641928)
XLA Ops:
  1.3 39.7 %shard_map.104 = (f32[384,128]{1,0:T(8,128)S(1)}, f32[24,128]{1,0:T(8,128)S(1)}) custom-call(s32[1,1]{1,0:T(1,128)S(6)} %copy.17.counts, s32[2,12]{1,0:T(2,128)} %bitcast.14, s32[1,12]{1,0:T(1,128)} %bitcast.15, s32[2]{0:T(128)} %window_in.1, f32[384,128]{1,0:T(8,128)} %bitcast.12, f32[24,128]{1,0:T(8,128)} %bitcast.13, bf16[2,64,64]{2,1,0:T(8,128)(2,1)} %back_in.1, ...), custom_call_target="tpu_custom_call" | custom-call | tf_op jit(solution)/shard_map/pallas_call | solution.py:686
  41.0 0.7 %copy.18 = f32[1,1,12,4096]{3,1,2,0:T(1,128)} copy(f32[1,1,12,4096]{3,1,2,0:T(1,128)S(1)} %bitcast.9) | data formatting | bytes 393216
  41.6 0.6 %copy.19 = f32[1,1,12,256]{3,1,2,0:T(1,128)} copy(f32[1,1,12,256]{3,1,2,0:T(1,128)S(1)} %bitcast.10) | data formatting | bytes 24576

commit v8 on v7

--- a/solution.py
+++ b/solution.py
@@ -72,9 +72,9 @@
     counts, anchors_in, groups_in, window_in, footprints_in, temporal_in, back_in, back_time_in, movie_in,
     out_shapes, out_traces,
     anchors, groups, window, footprints, temporal, back_raw, back_time, movie, back_even, back, pad_f, hl, code, code_right, r_code, cm, r_cm, near_cm, target, canvas, x3,
-    shares, share_out, r_share, wave, r_wave, call_f, c_high, c_low, temp, dense, labels, far_f, near_f,
-    r_mate, mate_cm, mate_goal, mate_v, mate_wave, r_far, mate_f, mate_high, mate_low,
-    joint, r_joint, outer, r_outer, outer_wave, outer_f, outer_high, outer_low,
+    shares, share_out, r_share, wave, r_wave, call_f, temp, dense, labels, far_f, near_f,
+    r_mate, mate_cm, mate_goal, mate_v, mate_wave, r_far, mate_f,
+    joint, r_joint, outer, r_outer, outer_wave, outer_f,
     piece_up, r_piece, merged, r_merged,
     load_sem, cm_send, cm_recv, r_send, r_recv, s_send, s_recv, t_send, t_recv, p_send, p_recv, m_send, m_recv,
     mate_send, mate_recv, mw_send, far_send, far_recv, joint_sem, outer_sem, ow_send,
@@ -164,7 +164,7 @@
             for g in range(2):
                 r_far[g, 1 + down] = jnp.zeros((8, 128), F32)
 
-    for ref in (call_f, c_high, c_low, far_f, near_f, mate_f, mate_high, mate_low, outer_f, outer_high, outer_low):
+    for ref in (far_f, near_f, mate_f, outer_f):
         ref[...] = jnp.zeros_like(ref)
 
     for load in loads[:4]:
@@ -430,31 +430,26 @@
         v = jnp.concatenate([part[:, FRAMES : FRAMES + NEAR] for part in parts], axis=1) * scale
         return total[:, :FRAMES] * scale, v
 
-    def stacked(v):
-        return jnp.concatenate(split(v), axis=0)
+    def weights(v, g):
+        high, low = split(jnp.concatenate([v[:, k * NEAR + g * PAD : k * NEAR + g * PAD + PAD] for k in range(4)], axis=1))
+        return jnp.concatenate([high, high, low], axis=1)
 
     goal, v_own = joined([share_out[3], r_share[2], r_share[1], r_share[0]], live_own)
-    v_both = stacked(v_own)
+    v_parts = [weights(v_own, g) for g in range(3)]
     own = cm[:, :FRAMES]
     row_group = lax.broadcasted_iota(I32, (PAD, FRAMES), 0) >> 2
 
-    def changes(sources, g, full, high_ref, low_ref):
+    def changes(sources, full):
         for k in range(4):
             for t in range(4):
                 if TILE_SETS[k][t] not in sources:
                     continue
                 new = sources[TILE_SETS[k][t]]
-                at = slice(k * NEAR + g * PAD + t * 4, k * NEAR + g * PAD + t * 4 + 4)
+                at = slice(k * PAD + t * 4, k * PAD + t * 4 + 4)
                 full[at, :128] = new[:4, :]
                 full[at, 128:] = new[4:, :]
-            at = slice(k * NEAR + g * PAD, k * NEAR + g * PAD + PAD)
-            high, low = split(full[at, :])
-            high_ref[at, :] = high
-            low_ref[at, :] = low
-
-    def remaining(aim, v_two, high_ref, low_ref):
-        product = mm(v_two, high_ref[...])
-        return aim - (product[:PAD] + product[PAD:] + mm(v_two[:PAD], low_ref[...]))
+        high, low = split(full[...])
+        return jnp.concatenate([high, low, high], axis=0)
 
     def updated(g, left_over, old, live):
         chosen = (row_group == g) & (live > 0)
@@ -513,8 +508,8 @@
             start(mate_copy(g, 0, UP, under), role & there(UP))
             start(mate_copy(g, 1, DOWN, over), role & there(DOWN))
 
+    left_over = goal
     for g in range(GROUPS):
-        left_over = goal
         if g == GROUPS - 1:
             arrived(remote(merged, r_merged, m_send, m_recv, RIGHT), there(RIGHT))
             spot = lax.broadcasted_iota(I32, (PAD, PIX), 1)
@@ -549,8 +544,7 @@
                 def _():
                     sources = {d: r_wave[0, d] for d in (UP, DOWN, LEFT, UL, DL)}
                     sources[OWN] = wave[0]
-                    changes(sources, 0, mate_f, mate_high, mate_low)
-                    aim = jnp.where(live_own > 0, remaining(goal, v_both, mate_high, mate_low), own)
+                    aim = jnp.where(live_own > 0, goal - mm(v_parts[0], changes(sources, mate_f)), own)
                     for at, value in enumerate((aim, own, v_own)):
                         outer[at, :4, :] = value[4:8, :128]
                         outer[at, 4:, :] = value[4:8, 128:]
@@ -562,8 +556,8 @@
                 if g - 1 >= first:
                     arrived(mate_copy(g - 1, 0, UP, over), role & there(UP))
                     arrived(mate_copy(g - 1, 1, DOWN, under), role & there(DOWN))
-            changes({**{d: r_wave[g - 1, d] for d in range(8)}, OWN: wave[g - 1]}, g - 1, call_f, c_high, c_low)
-            left_over = remaining(goal, v_both, c_high, c_low)
+            around = {**{d: r_wave[g - 1, d] for d in range(8)}, OWN: wave[g - 1]}
+            left_over = left_over - mm(v_parts[g - 1], changes(around, call_f))
         new = updated(g, left_over, own, live_own)
         if g < GROUPS - 1:
             pack(wave, g, new, own)
@@ -596,7 +590,8 @@
                 r_mate[1] = share_out[2]
                 live = mate_cm[:, FRAMES + 2 : FRAMES + 3]
                 mate_goal[...], v_mate = joined([r_mate[k] for k in range(4)], live)
-                mate_v[...] = stacked(v_mate)
+                for k in range(2):
+                    mate_v[k] = weights(v_mate, k)
                 old = mate_cm[:, :FRAMES]
                 pack(mate_wave, 0, updated(0, mate_goal[...], old, live), old)
 
@@ -624,7 +619,8 @@
                 def _():
                     mate_cm[...] = r_cm[RIGHT]
                     mate_goal[...] = r_joint[:, :FRAMES]
-                    mate_v[...] = stacked(r_joint[:, FRAMES:])
+                    for k in range(2):
+                        mate_v[k] = weights(r_joint[:, FRAMES:], k)
 
             for down in (-1, 0, 1):
                 arrived(far_copy(g - 1, -down, -2), west & row_ok(down))
@@ -640,10 +636,10 @@
                         sources[tile] = wave[g - 1] if at == OWN else r_wave[g - 1, at]
                     for down, tile in enumerate(far_at):
                         sources[tile] = r_far[g - 1, down]
-                    changes(sources, g - 1, mate_f, mate_high, mate_low)
                     old = mate_cm[:, :FRAMES]
                     live = mate_cm[:, FRAMES + 2 : FRAMES + 3]
-                    rest = remaining(mate_goal[...], mate_v[...], mate_high, mate_low)
+                    rest = mate_goal[...] - mm(mate_v[g - 1], changes(sources, mate_f))
+                    mate_goal[...] = rest
                     pack(mate_wave, g, updated(g, rest, old, live), old)
 
             start_mate(g)
@@ -652,7 +648,7 @@
 
                 @pl.when(east)
                 def _():
-                    changes({UR: r_wave[0, UL], RIGHT: r_wave[0, LEFT], DR: r_wave[0, DL]}, 0, outer_f, outer_high, outer_low)
+                    rhs = changes({UR: r_wave[0, UL], RIGHT: r_wave[0, LEFT], DR: r_wave[0, DL]}, outer_f)
                     zero = jnp.zeros((4, FRAMES), F32)
                     aim, old, v = (
                         jnp.concatenate(
@@ -660,7 +656,7 @@
                         )
                         for at in range(3)
                     )
-                    value = jnp.maximum(remaining(aim, stacked(v), outer_high, outer_low), 0.0)
+                    value = jnp.maximum(aim - mm(weights(v, 0), rhs), 0.0)
                     pack2 = value - old
                     outer_wave[:4, :] = pack2[4:8, :128]
                     outer_wave[4:, :] = pack2[4:8, 128:]
@@ -718,9 +714,7 @@
             pltpu.VMEM((3, PAD, FRAMES + 128), F32),
             pltpu.VMEM((3, 8, 128), F32),
             pltpu.VMEM((3, 8, 8, 128), F32),
-            pltpu.VMEM((4 * NEAR, FRAMES), F32),
-            pltpu.VMEM((4 * NEAR, FRAMES), BF16),
-            pltpu.VMEM((4 * NEAR, FRAMES), BF16),
+            pltpu.VMEM((4 * PAD, FRAMES), F32),
             pltpu.VMEM((PAD, PIX), F32),
             pltpu.VMEM((DENSE, WIDE), F32),
             pltpu.VMEM((DENSE, 128), F32),
@@ -729,20 +723,16 @@
             pltpu.VMEM((4, PAD, FRAMES + 128), F32),
             pltpu.VMEM((PAD, FRAMES + 128), F32),
             pltpu.VMEM((PAD, FRAMES), F32),
-            pltpu.VMEM((2 * PAD, 4 * NEAR), BF16),
+            pltpu.VMEM((2, PAD, 3 * NEAR), BF16),
             pltpu.VMEM((3, 8, 128), F32),
             pltpu.VMEM((2, 3, 8, 128), F32),
-            pltpu.VMEM((4 * NEAR, FRAMES), F32),
-            pltpu.VMEM((4 * NEAR, FRAMES), BF16),
-            pltpu.VMEM((4 * NEAR, FRAMES), BF16),
+            pltpu.VMEM((4 * PAD, FRAMES), F32),
             pltpu.VMEM((PAD, 2 * FRAMES), F32),
             pltpu.VMEM((PAD, 2 * FRAMES), F32),
             pltpu.VMEM((3, 8, 128), F32),
             pltpu.VMEM((3, 8, 128), F32),
             pltpu.VMEM((8, 128), F32),
-            pltpu.VMEM((4 * NEAR, FRAMES), F32),
-            pltpu.VMEM((4 * NEAR, FRAMES), BF16),
-            pltpu.VMEM((4 * NEAR, FRAMES), BF16),
+            pltpu.VMEM((4 * PAD, FRAMES), F32),
             pltpu.VMEM((2, DENSE, WIDE), I16),
             pltpu.VMEM((2, DENSE, WIDE), I16),
             pltpu.VMEM((DENSE, WIDE), I16),

time: 42.3 us -> 42.3 us (level)
  no operation moved by 1% of the time
where the time goes in v8:
time: 42.3 us; the launch traced here: 42.2 us
  Pallas kernels  39.6 us (94%)
  between operations  1.29 us (3%)
  local copies, waits for them, and re-layouts  1.28 us (3%)
    pallas_call x1, Pallas kernels, on_device(): pl.pallas_call(functools.partial(kernel, rows, cols), out_shape=(jax.Shap...  39.6 us
    unnamed x2, local copies, waits for them, and re-layouts  1.28 us

profile of v8, /device:TPU:7, one launch (start us, length us, event | category | flops | bytes accessed | tf_op | source)
XLA Modules:
  0.0 42.2 jit_solution(4720235365455631451)
XLA Ops:
  1.3 39.6 %shard_map.104 = (f32[384,128]{1,0:T(8,128)S(1)}, f32[24,128]{1,0:T(8,128)S(1)}) custom-call(s32[1,1]{1,0:T(1,128)S(6)} %copy.17.counts, s32[2,12]{1,0:T(2,128)} %bitcast.14, s32[1,12]{1,0:T(1,128)} %bitcast.15, s32[2]{0:T(128)} %window_in.1, f32[384,128]{1,0:T(8,128)} %bitcast.12, f32[24,128]{1,0:T(8,128)} %bitcast.13, bf16[2,64,64]{2,1,0:T(8,128)(2,1)} %back_in.1, ...), custom_call_target="tpu_custom_call" | custom-call | tf_op jit(solution)/shard_map/pallas_call | solution.py:682
  40.9 0.7 %copy.18 = f32[1,1,12,4096]{3,1,2,0:T(1,128)} copy(f32[1,1,12,4096]{3,1,2,0:T(1,128)S(1)} %bitcast.9) | data formatting | bytes 393216
  41.6 0.6 %copy.19 = f32[1,1,12,256]{3,1,2,0:T(1,128)} copy(f32[1,1,12,256]{3,1,2,0:T(1,128)S(1)} %bitcast.10) | data formatting | bytes 24576

commit v9 on v8

--- a/solution.py
+++ b/solution.py
@@ -665,7 +665,9 @@
                 start(outer_copy(0, UP), east & there(UP))
                 start(outer_copy(2, DOWN), east & there(DOWN))
 
-    back_own = jnp.dot(unpick16, own, precision=lax.Precision.HIGHEST, preferred_element_type=F32)
+    high, low = split(own)
+    least = (own - high.astype(F32) - low.astype(F32)).astype(BF16)
+    back_own = mm(jnp.concatenate([unpick16] * 3, axis=1).astype(BF16), jnp.concatenate([high, low, least], axis=0))
     new_traces = jnp.where(alive_sub[:SLOTS, 0:1], back_own[:SLOTS, :], old_traces)
     for half in range(2):
         out_traces[pl.ds(half, SLOTS, stride=2), :] = new_traces[:, half * 128 : half * 128 + 128]

time: 42.3 us -> 42.3 us (level)
  no operation moved by 1% of the time
where the time goes in v9:
time: 42.3 us; the launch traced here: 42.2 us
  Pallas kernels  39.6 us (94%)
  between operations  1.29 us (3%)
  local copies, waits for them, and re-layouts  1.28 us (3%)
    pallas_call x1, Pallas kernels, on_device(): pl.pallas_call(functools.partial(kernel, rows, cols), out_shape=(jax.Shap...  39.6 us
    unnamed x2, local copies, waits for them, and re-layouts  1.28 us

profile of v9, /device:TPU:7, one launch (start us, length us, event | category | flops | bytes accessed | tf_op | source)
XLA Modules:
  0.0 42.2 jit_solution(16773393633076801579)
XLA Ops:
  1.3 39.6 %shard_map.104 = (f32[384,128]{1,0:T(8,128)S(1)}, f32[24,128]{1,0:T(8,128)S(1)}) custom-call(s32[1,1]{1,0:T(1,128)S(6)} %copy.17.counts, s32[2,12]{1,0:T(2,128)} %bitcast.14, s32[1,12]{1,0:T(1,128)} %bitcast.15, s32[2]{0:T(128)} %window_in.1, f32[384,128]{1,0:T(8,128)} %bitcast.12, f32[24,128]{1,0:T(8,128)} %bitcast.13, bf16[2,64,64]{2,1,0:T(8,128)(2,1)} %back_in.1, ...), custom_call_target="tpu_custom_call" | custom-call | tf_op jit(solution)/shard_map/pallas_call | solution.py:684
  40.9 0.7 %copy.18 = f32[1,1,12,4096]{3,1,2,0:T(1,128)} copy(f32[1,1,12,4096]{3,1,2,0:T(1,128)S(1)} %bitcast.9) | data formatting | bytes 393216
  41.6 0.6 %copy.19 = f32[1,1,12,256]{3,1,2,0:T(1,128)} copy(f32[1,1,12,256]{3,1,2,0:T(1,128)S(1)} %bitcast.10) | data formatting | bytes 24576
